TPU v7x, 256 devices: a whole 4x4x8 slice. The times are simulated.
256 devices in a mesh: dp: 8 (over x, core), shard: 32 (over z, y).
Axes of the slice: x: 4, y: 4, z: 8, core: 2. Of those that a mesh axis runs over, the one named last changes fastest.
Arguments:
- table: float32 [65536, 128], P('shard'), may hold values from -6 to 6
- cross_weight: bfloat16 [1024, 1024], replicated, may hold values from -0.1875 to 0.1875
- cross_bias: float32 [1024], replicated, may hold values from -3 to 3
- top_weight: bfloat16 [1024, 512], replicated, may hold values from -0.1875 to 0.1875
- top_bias: float32 [512], replicated, may hold values from -3 to 3
- out_weight: float32 [512], replicated, may hold values from -0.25 to 0.25
- wanted: int32 [256, 32, 128], P(('dp', 'shard')), may hold values from 0 to 2047, as said below
- slots: int32 [131072, 8, 4], P(('dp', 'shard')), may hold values from 0 to 4095
- lengths: int32 [131072, 8], P(('dp', 'shard')), may hold values from 1 to 4
- logit_grad: float32 [131072], P(('dp', 'shard')), may hold values from -6 to 6
Outputs:
- logits: float32 [131072], P(('dp', 'shard'))
- grad_cross: float32 [1024, 1024], replicated
- grad_top: float32 [1024, 512], replicated
- grad_cross_bias: float32 [1024], replicated
- grad_top_bias: float32 [512], replicated
- grad_out: float32 [512], replicated
- table_grad: float32 [65536, 128], P('shard')
Inputs may be any that keep to these rules, and one draw needn't show every extreme that they name: `wanted`: the 128 rows that one device fetches from one owner are distinct.
All inputs are finite; a program needn't handle non-finite values.
Results may differ from a plain program's by a relative error of at most 0.0084.
Values sent between devices are 32-bit elements; how exact they have to be, the bound alone decides.
A program may use at most 128 MiB of HBM per device.

v0:
```python
import jax
import jax.numpy as jnp
from jax import lax
from jax.sharding import PartitionSpec as P


def on_device(
    table,
    cross_weight,
    cross_bias,
    top_weight,
    top_bias,
    out_weight,
    wanted,
    slots,
    lengths,
    logit_grad,
):
    emb = table.shape[1]
    samples = slots.shape[0]
    feats = slots.shape[1]
    bag = slots.shape[2]
    requests = wanted[0]
    served = lax.all_to_all(requests, "shard", split_axis=0, concat_axis=0, tiled=True)
    cache = lax.all_to_all(
        jnp.take(table, served, axis=0), "shard", split_axis=0, concat_axis=0, tiled=True
    )
    cache_flat = cache.reshape(-1, emb)
    live = (jnp.arange(bag, dtype=jnp.int32)[None, None, :] < lengths[:, :, None]).astype(
        jnp.float32
    )
    gathered = cache_flat[slots]
    pooled = jnp.sum(gathered * live[..., None], axis=2)
    x0 = pooled.reshape(samples, feats * emb).astype(jnp.bfloat16)
    xfull = x0.astype(jnp.float32)
    yval = jnp.dot(x0, cross_weight, preferred_element_type=jnp.float32) + cross_bias
    hidden = (xfull * yval + xfull).astype(jnp.bfloat16)
    zval = jnp.dot(hidden, top_weight, preferred_element_type=jnp.float32) + top_bias
    sig = jax.nn.sigmoid(zval)
    uval = zval * sig
    logits = jnp.dot(uval, out_weight, precision=lax.Precision.HIGHEST)
    g_out = jnp.dot(logit_grad, uval, precision=lax.Precision.HIGHEST)
    dz = logit_grad[:, None] * out_weight[None, :] * (sig * (1.0 + zval * (1.0 - sig)))
    dzb = dz.astype(jnp.bfloat16)
    g_top = jnp.dot(hidden.T, dzb, preferred_element_type=jnp.float32)
    g_tbias = jnp.sum(dz, axis=0)
    dh = jnp.dot(dzb, top_weight.T, preferred_element_type=jnp.float32)
    dy = dh * xfull
    dyb = dy.astype(jnp.bfloat16)
    g_cross = jnp.dot(x0.T, dyb, preferred_element_type=jnp.float32)
    g_cbias = jnp.sum(dy, axis=0)
    dx = dh * (yval + 1.0) + jnp.dot(dyb, cross_weight.T, preferred_element_type=jnp.float32)
    contrib = dx.reshape(samples, feats, 1, emb) * live[..., None]
    slot_grads = (
        jnp.zeros(cache_flat.shape, jnp.float32).at[slots.reshape(-1)].add(contrib.reshape(-1, emb))
    )
    returned = lax.all_to_all(
        slot_grads.reshape(cache.shape), "shard", split_axis=0, concat_axis=0, tiled=True
    )
    owner_grad = (
        jnp.zeros(table.shape, jnp.float32).at[served.reshape(-1)].add(returned.reshape(-1, emb))
    )
    table_grad = lax.psum(owner_grad, "dp")
    summed = lax.psum((g_cross, g_top, g_cbias, g_tbias, g_out), ("dp", "shard"))
    return (logits, summed[0], summed[1], summed[2], summed[3], summed[4], table_grad)


def solution(mesh):
    placed = (
        P("shard", None),
        P(),
        P(),
        P(),
        P(),
        P(),
        P(("dp", "shard"), None, None),
        P(("dp", "shard"), None, None),
        P(("dp", "shard"), None),
        P(("dp", "shard")),
    )
    return jax.shard_map(
        on_device,
        mesh=mesh,
        in_specs=placed,
        out_specs=(P(("dp", "shard")), P(), P(), P(), P(), P(), P("shard", None)),
        check_vma=False,
    )
```

profile of v0, /device:TPU:1, one launch (start us, length us, event | category | flops | bytes accessed | tf_op | source)
XLA Modules:
  0.0 659.6 jit_solution(8032694361163079819)
XLA Ops:
  7.2 0.0 copy-start
  7.2 0.0 copy-start.1
  7.2 12.3 %all-to-all-start = ((s32[32,1,128]{2,1,0:T(1,128)}), s32[32,1,128]{2,1,0:T(1,128)S(1)}, u32[]{:S(2)}, u32[]{:S(2)}) async-start(s32[32,1,128]{2,1,0:T(1,128)} %bitcast.60), calls=%async_computation | async-start | bytes 32768 | tf_op jit(solution)/shard_map/all_to_all | solution.py:24
  19.5 0.8 copy.22
  20.4 2.6 fusion.4
  23.0 5.1 all-to-all-done
  28.0 0.0 copy-done.1
  28.1 14.2 %gather_fusion = f32[4096,128]{1,0:T(8,128)} fusion(f32[2048,128]{1,0:T(8,128)S(1)} %copy-done.1, s32[4096]{0:T(1024)S(1)} %fusion.30), kind=kCustom, calls=%fused_computation | custom fusion | bytes 4210688 | tf_op jit(solution)/shard_map/jit(_take)/gather | solution.py:26
  42.3 2.9 broadcast_select_fusion
  45.1 4.9 all-to-all-start.1
  50.1 0.0 copy-done.6
  50.1 2.0 copy.23
  52.1 3.2 reshape.150
  55.3 2.0 copy.21
  57.3 3.2 reshape.161
  60.5 3.3 reshape.147
  63.8 0.1 compare_select_fusion
  63.9 33.0 %all-to-all-done.1 = f32[32,128,128]{2,1,0:T(8,128)} async-done(((f32[32,128,128]{2,1,0:T(8,128)}), f32[32,128,128]{2,1,0:T(8,128)}, u32[]{:S(2)}, u32[]{:S(2)}) %all-to-all-start.1) | async-done | bytes 2097184 | tf_op jit(solution)/shard_map/all_to_all | solution.py:25
  96.9 56.1 %gather_fusion.1 = f32[16384,128]{1,0:T(8,128)} fusion(f32[4096,128]{1,0:T(8,128)} %bitcast.5, s32[16384]{0:T(1024)S(1)} %broadcast_clamp_fusion), kind=kCustom, calls=%fused_computation.1 | custom fusion | bytes 16842752 | tf_op jit(solution)/shard_map/gather | solution.py:32
  153.0 8.0 %multiply_reduce_fusion = bf16[512,8,128]{2,1,0:T(8,128)(2,1)S(1)} fusion(f32[512,8,4,128]{3,2,1,0:T(4,128)} %bitcast.48, f32[512,8,4]{2,1,0:T(8,128)} %fusion.4), kind=kLoop, calls=%fused_computation.6 | loop fusion | flops 3670016 | bytes 9502720 | tf_op jit(solution)/shard_map/reduce_sum | solution.py:33
  161.0 0.0 copy-done
  161.0 0.0 copy-done.8
  161.0 0.0 copy-start.7
  161.1 0.0 copy-start.9
  161.1 0.0 copy-start.10
  161.1 0.0 copy-start.11
  161.1 1.4 fusion.3
  162.5 0.0 copy-start.14
  162.5 0.0 copy-done.7
  162.5 0.0 copy-done.9
  162.5 0.0 copy-done.10
  162.5 0.0 copy-done.11
  162.5 1.0 fusion.33
  163.5 0.0 copy-done.14
  163.5 0.0 copy-start.12
  163.5 1.1 fusion.5
  164.6 0.0 copy-done.12
  164.6 0.0 copy-start.2
  164.6 1.3 add_bitcast_fusion
  166.0 0.0 copy-done.2
  166.0 1.8 copy.25
  167.7 7.4 %mul.73 = f32[512,8,4,128]{3,2,1,0:T(4,128)} broadcast(f32[512,8,128]{2,1,0:T(8,128)} %bitcast.54), dimensions={0,1,3} | broadcast | bytes 10485760 | tf_op jit(solution)/shard_map/mul | solution.py:53
  175.1 97.5 %scatter_custom_fusion = f32[4096,128]{1,0:T(8,128)} fusion(s32[16384]{0:T(1024)S(1)} %bitcast.59, f32[16384,128]{1,0:T(8,128)} %bitcast.49, f32[16384]{0:T(1024)S(1)} %reshape.150, f32[]{:T(128)} %constant.12.clone.1), kind=kCustom, calls=%fused_computation.4 | custom fusion | flops 4194304 | bytes 10551300 | tf_op jit(solution)/shard_map/scatter-add | solution.py:55
  272.6 7.5 %all-to-all-start.2 = ((f32[32,128,128]{2,1,0:T(8,128)}), f32[32,128,128]{2,1,0:T(8,128)}, u32[]{:S(2)}, u32[]{:S(2)}) async-start(f32[32,128,128]{2,1,0:T(8,128)} %bitcast.55), calls=%async_computation.2 | async-start | bytes 4194304 | tf_op jit(solution)/shard_map/all_to_all | solution.py:57
  280.1 0.0 all-reduce.7.cloned.1.call-start
  280.1 0.0 copy-start.3
  280.2 4.0 fusion.21
  284.1 0.0 copy-done.3
  284.1 3.3 fusion.8
  287.5 0.0 all-reduce.7.cloned.1.call-update
  287.5 0.0 copy-start.13
  287.5 0.0 all-reduce.5.cloned.1.call-start
  287.6 43.0 %all-to-all-done.2 = f32[32,128,128]{2,1,0:T(8,128)} async-done(((f32[32,128,128]{2,1,0:T(8,128)}), f32[32,128,128]{2,1,0:T(8,128)}, u32[]{:S(2)}, u32[]{:S(2)}) %all-to-all-start.2) | async-done | bytes 2097184 | tf_op jit(solution)/shard_map/all_to_all | solution.py:57
  330.6 23.9 %scatter_custom_fusion.1 = f32[2048,128]{1,0:T(8,128)} fusion(s32[4096]{0:T(1024)S(1)} %bitcast.61, f32[4096,128]{1,0:T(8,128)} %bitcast.16, f32[]{:T(128)} %constant.12.clone.1), kind=kCustom, calls=%fused_computation.30 | custom fusion | flops 524288 | bytes 1049088 | tf_op jit(solution)/shard_map/scatter-add | solution.py:61
  354.4 0.0 all-reduce.5.cloned.1.call-update
  354.5 0.9 fusion.25
  355.3 81.0 %all-reduce = (f32[1024]{0:T(1024)}, f32[512]{0:T(512)}, f32[512]{0:T(512)}) all-reduce(f32[1024]{0:T(1024)S(1)} %get-tuple-element.14, f32[512]{0:T(512)S(1)} %get-tuple-element.16, f32[512]{0:T(512)S(1)} %bitcast.62), channel_id=1, replica_groups=mesh['dp'=8,'shard'=32] {'dp','shard'}, use_global_device_ids=true, to_apply=%region_4.5 | all-reduce | flops 2048 | bytes 16384 | tf_op jit(solution)/shard_map/psum | solution.py:64
  436.3 1.8 fusion.27
  438.1 138.1 %all-reduce.7.cloned.1.call-done = (f32[1024,1024]{1,0:T(8,128)}, f32[1024,512]{1,0:T(8,128)}) async-done(((f32[1024,1024]{1,0:T(8,128)}, f32[1024,512]{1,0:T(8,128)}), (f32[1024,1024]{1,0:T(8,128)}, f32[1024,512]{1,0:T(8,128)})) %all-reduce.7.cloned.1.call-update) | async-done | bytes 6291472 | tf_op jit(solution)/shard_map/psum | solution.py:64
  576.3 68.7 %all-reduce.5.cloned.1.call-done = f32[2048,128]{1,0:T(8,128)} async-done(((f32[2048,128]{1,0:T(8,128)}), f32[2048,128]{1,0:T(8,128)}) %all-reduce.5.cloned.1.call-update) | async-done | bytes 1048592 | tf_op jit(solution)/shard_map/psum | solution.py:63
  644.9 4.9 copy.47
  649.9 1.3 copy.48
  651.2 0.6 copy-done.5
  651.8 1.0 copy.49
  (11 shorter events, 0.1 us)
Async XLA Ops:
  7.2 153.9 %copy-start = (bf16[1024,1024]{1,0:T(8,128)(2,1)S(1)}, bf16[1024,1024]{1,0:T(8,128)(2,1)}, u32[]{:S(2)}) copy-start(bf16[1024,1024]{1,0:T(8,128)(2,1)} %param.11) | copy-start | bytes 6291460
  7.2 20.9 %copy-start.1 = (f32[2048,128]{1,0:T(8,128)S(1)}, f32[2048,128]{1,0:T(8,128)}, u32[]{:S(2)}) copy-start(f32[2048,128]{1,0:T(8,128)} %param.10) | copy-start | bytes 3145732
  7.2 20.8 %all-to-all-start = ((s32[32,1,128]{2,1,0:T(1,128)}), s32[32,1,128]{2,1,0:T(1,128)S(1)}, u32[]{:S(2)}, u32[]{:S(2)}) async-start(s32[32,1,128]{2,1,0:T(1,128)} %bitcast.60), calls=%async_computation | async-start | bytes 32768 | tf_op jit(solution)/shard_map/all_to_all | solution.py:24
  45.1 4.9 copy-start.6
  45.1 51.8 %all-to-all-start.1 = ((f32[32,128,128]{2,1,0:T(8,128)}), f32[32,128,128]{2,1,0:T(8,128)}, u32[]{:S(2)}, u32[]{:S(2)}) async-start(f32[32,128,128]{2,1,0:T(8,128)} %broadcast_select_fusion), calls=%async_computation.1 | async-start | bytes 4194304 | tf_op jit(solution)/shard_map/all_to_all | solution.py:25
  153.0 8.1 %copy-start.8 = (f32[1024]{0:T(1024)S(1)}, f32[1024]{0:T(1024)}, u32[]{:S(2)}) copy-start(f32[1024]{0:T(1024)} %param.12) | copy-start | bytes 12292
  161.0 1.4 copy-start.7
  161.1 1.4 copy-start.9
  161.1 1.4 copy-start.10
  161.1 1.4 copy-start.11
  162.5 1.1 copy-start.14
  163.5 1.1 copy-start.12
  164.6 1.3 copy-start.2
  272.6 58.0 %all-to-all-start.2 = ((f32[32,128,128]{2,1,0:T(8,128)}), f32[32,128,128]{2,1,0:T(8,128)}, u32[]{:S(2)}, u32[]{:S(2)}) async-start(f32[32,128,128]{2,1,0:T(8,128)} %bitcast.55), calls=%async_computation.2 | async-start | bytes 4194304 | tf_op jit(solution)/shard_map/all_to_all | solution.py:57
  280.1 296.2 %all-reduce.7.cloned.1.call-start = ((), (), s32[]{:S(2)}) async-start(), calls=%async_computation.4 | async-start | bytes 12582912 | tf_op jit(solution)/shard_map/psum | solution.py:64
  280.1 4.0 copy-start.3
  287.5 67.0 %copy-start.13 = (f32[512,512]{1,0:T(8,128)S(1)}, f32[512,512]{1,0:T(8,128)}, u32[]{:S(2)}) copy-start(f32[512,512]{1,0:T(8,128)} %copy-done.12) | copy-start | bytes 3145732
  287.5 357.5 %all-reduce.5.cloned.1.call-start = ((), (), s32[]{:S(2)}) async-start(), calls=%async_computation.3 | async-start | bytes 2097152 | tf_op jit(solution)/shard_map/psum | solution.py:63
  644.9 4.9 copy-start.4
  649.9 2.0 copy-start.5
Sparse Core Ops, SparseCore 0:
  287.6 288.6 all-reduce.6
  579.3 65.5 all-reduce.4
where the time goes:
time: 661 us; the launch traced here: 660 us
  waiting for transfers between devices  288 us (44%)
  other arithmetic  135 us (20%)
  local copies, waits for them, and re-layouts  102 us (15%)
  blocking collectives  81 us (12%)
  starting transfers between devices  24.8 us (4%)
  matrix products  14.7 us (2%)
  between operations  14.4 us (2%)
    psum x1, waiting for transfers between devices, on_device(): lax.psum((g_cross, g_top, g_cbias, g_tbias, g_out), ('dp', 'shard'))  138 us
    scatter-add x1, other arithmetic, on_device(): jnp.zeros(cache_flat.shape, jnp.float32).at[slots.reshape(-1)]  97.5 us
    psum x1, blocking collectives, on_device(): lax.psum((g_cross, g_top, g_cbias, g_tbias, g_out), ('dp', 'shard'))  81 us
    psum x1, waiting for transfers between devices, on_device(): table_grad = lax.psum(owner_grad, 'dp')  68.7 us
    gather x1, local copies, waits for them, and re-layouts, on_device(): gathered = cache_flat[slots]  56.1 us
    all_to_all x1, waiting for transfers between devices, on_device(): lax.all_to_all(slot_grads.reshape(cache.shape), 'shard', split_axis=0, co...  43 us
    all_to_all x1, waiting for transfers between devices, on_device(): lax.all_to_all(jnp.take(table, served, axis=0), 'shard', split_axis=0, co...  33 us
    scatter-add x1, other arithmetic, on_device(): jnp.zeros(table.shape, jnp.float32).at[served.reshape(-1)]  23.9 us
  transfers between devices with their start and end apart: 5, of which 5 were waited for; matrix products, arithmetic and copies ran while one was open for 8% of the time, Pallas kernels for 0%

commit v1 on v0

v1 whole, which is shorter than its diff:
```python
import functools
import jax
import jax.numpy as jnp
from jax import lax
from jax.experimental import pallas as pl
from jax.experimental.pallas import tpu as pltpu
from jax.sharding import PartitionSpec as P

VMEM_BIG = 60 * 1024 * 1024


def peer_of(k, me, ny, nz):
    j = k // ny
    dz = nz // 2 + (j // 2 + j % 2) * (1 - 2 * (j % 2))
    dy = (k + 1) % ny
    z = (me // ny + dz + nz) % nz
    y = (me % ny + dy) % ny
    return z * ny + y


def fetch_kernel(n, ny, wanted, table, cache, ids_in, ids_sm, sendbuf,
                 id_send, id_recv, row_send, row_recv, sm_sem):
    nz = n // ny
    cap = wanted.shape[2]
    me = lax.axis_index("shard")
    barrier = pltpu.get_barrier_semaphore()

    @pl.loop(0, n - 1)
    def _(k):
        pl.semaphore_signal(barrier, inc=1, device_id={"shard": peer_of(k, me, ny, nz)})

    pl.semaphore_wait(barrier, n - 1)

    def id_copy(p):
        return pltpu.make_async_remote_copy(
            src_ref=wanted.at[p], dst_ref=ids_in.at[me], send_sem=id_send.at[p],
            recv_sem=id_recv.at[me], device_id={"shard": p})

    def id_arrival(p):
        return pltpu.make_async_remote_copy(
            src_ref=wanted.at[p], dst_ref=ids_in.at[p], send_sem=id_send.at[p],
            recv_sem=id_recv.at[p], device_id={"shard": p})

    def row_copy(p):
        return pltpu.make_async_remote_copy(
            src_ref=sendbuf.at[p], dst_ref=cache.at[me], send_sem=row_send.at[p],
            recv_sem=row_recv.at[me], device_id={"shard": p})

    def row_arrival(p):
        return pltpu.make_async_remote_copy(
            src_ref=sendbuf.at[p], dst_ref=cache.at[p], send_sem=row_send.at[p],
            recv_sem=row_recv.at[p], device_id={"shard": p})

    @pl.loop(0, n - 1)
    def _(k):
        id_copy(peer_of(k, me, ny, nz)).start()

    ids_in[me] = wanted[me]

    @pl.loop(0, n - 1)
    def _(k):
        id_arrival(peer_of(k, me, ny, nz)).wait_recv()

    to_smem = pltpu.make_async_copy(ids_in, ids_sm, sm_sem)
    to_smem.start()
    to_smem.wait()

    def serve(p, out):
        @pl.loop(0, cap // 16)
        def _(t):
            for i in range(16):
                row = t * 16 + i
                out[p, pl.ds(row, 1), :] = table[pl.ds(ids_sm[p, 0, row], 1), :]

    @pl.loop(0, n - 1)
    def _(k):
        p = peer_of(k, me, ny, nz)
        serve(p, sendbuf)
        row_copy(p).start()

    serve(me, cache)

    @pl.loop(0, n - 1)
    def _(k):
        p = peer_of(k, me, ny, nz)
        row_arrival(p).wait_recv()

    @pl.loop(0, n - 1)
    def _(k):
        p = peer_of(k, me, ny, nz)
        id_copy(p).wait_send()
        row_copy(p).wait_send()


def fetch(wanted, table, ny):
    n, cap = wanted.shape
    emb = table.shape[1]
    vm = pl.BlockSpec(memory_space=pltpu.VMEM)
    cache, served = pl.pallas_call(
        functools.partial(fetch_kernel, n, ny),
        out_shape=[
            jax.ShapeDtypeStruct((n, cap, emb), jnp.float32),
            jax.ShapeDtypeStruct((n, 1, cap), jnp.int32),
        ],
        in_specs=[vm, vm],
        out_specs=[vm, vm],
        scratch_shapes=[
            pltpu.SMEM((n, 1, cap), jnp.int32),
            pltpu.VMEM((n, cap, emb), jnp.float32),
            pltpu.SemaphoreType.DMA((n,)),
            pltpu.SemaphoreType.DMA((n,)),
            pltpu.SemaphoreType.DMA((n,)),
            pltpu.SemaphoreType.DMA((n,)),
            pltpu.SemaphoreType.DMA,
        ],
        compiler_params=pltpu.CompilerParams(
            collective_id=0, has_side_effects=True, vmem_limit_bytes=VMEM_BIG),
        name="fetch_rows",
    )(wanted.reshape(n, 1, cap), table)
    return cache, served

F32, BF16, I32 = jnp.float32, jnp.bfloat16, jnp.int32


def dot(a, b, dims):
    return lax.dot_general(a, b, (dims, ((), ())), preferred_element_type=F32)


NN = ((1,), (0,))
NT = ((1,), (1,))
TN = ((0,), (0,))


def split(x):
    hi = x.astype(BF16)
    lo = (x - hi.astype(F32)).astype(BF16)
    return jnp.concatenate([hi, lo], axis=1)


def nibble_scale(o):
    k = o % 8
    s = jnp.where((k & 1) == 1, F32(2.0**-4), F32(1.0))
    s = s * jnp.where((k & 2) == 2, F32(2.0**-8), F32(1.0))
    return s * jnp.where((k & 4) == 4, F32(2.0**-16), F32(1.0))


def key_codes(slots, lengths, b):
    slot = slots[:, b, :]
    owner = slot >> 7
    code = jnp.where(lengths[...] > b, (slot & 127) + ((owner >> 3) << 7), -1)
    return code, jnp.left_shift(jnp.ones_like(owner), (owner & 7) << 2)


def local_kernel(cache, slots, lengths, cot, cw, cb, tw, tb, ow,
                 logits, g_cross, g_top, g_cb, g_tb, g_ow, slot_grads,
                 words, wordst, colcode, colbit, rowcode, rowbit, acc, chl, x0, y, h, z, dzb, dyb, dh, dxhl):
    feats, bag, samples = slots.shape
    owners, cap, emb = cache.shape
    width, top = tw.shape
    groups = words.shape[0]

    for b in range(bag):
        code, bit = key_codes(slots, lengths, b)
        rowcode[pl.ds(b * feats, feats), :] = code
        rowbit[pl.ds(b * feats, feats), :] = bit
    colcode[...] = rowcode[...].T
    colbit[...] = rowbit[...].T

    lane = lax.broadcasted_iota(I32, (samples, cap), 1)
    for f in range(feats):
        sums = [jnp.zeros((samples, cap), I32)] * groups
        for b in range(bag):
            col = b * feats + f
            code = jnp.broadcast_to(colcode[:, col:col + 1], (samples, cap)) - lane
            bit = jnp.broadcast_to(colbit[:, col:col + 1], (samples, cap))
            for w in range(groups):
                sums[w] = sums[w] + jnp.where(code == w * cap, bit, 0)
        for w in range(groups):
            words[w, f] = sums[w]

    for o in range(owners):
        scale = 2.0 ** -(4 * (o % 8))
        chl[pl.ds(o * cap, cap), :] = split(cache[o] * scale)

    per = 4

    @pl.loop(0, owners // per)
    def _(g):
        w = g // 2
        rhs = chl[pl.ds(g * per * cap, per * cap), :]

        @pl.loop(0, feats)
        def _(f):
            word = words[w, f]
            tiles = []
            for i in range(per):
                mask = jnp.left_shift(jnp.int32(15), ((g % 2) * per + i) * 4)
                tiles.append((word & mask).astype(F32).astype(BF16))
            part = dot(jnp.concatenate(tiles, axis=1), rhs, NN)

            @pl.when(g == 0)
            def _():
                acc[f] = part

            @pl.when(g > 0)
            def _():
                acc[f] += part

    for f in range(feats):
        x0[:, f * emb:(f + 1) * emb] = (acc[f, :, :emb] + acc[f, :, emb:]).astype(BF16)

    step = 256

    @pl.loop(0, width // step)
    def _(j):
        c = pl.ds(pl.multiple_of(j * step, step), step)
        yv = dot(x0[...], cw[:, c], NN) + cb[:, c]
        y[:, c] = yv
        xf = x0[:, c].astype(F32)
        h[:, c] = (xf * yv + xf).astype(BF16)

    cotb = jnp.broadcast_to(cot[...], (128, samples)).T
    lsum = jnp.zeros((samples, 128), F32)
    for j in range(top // step):
        c = pl.ds(j * step, step)
        zv = dot(h[...], tw[:, c], NN) + tb[:, c]
        sig = jax.nn.sigmoid(zv)
        u = zv * sig
        uw = u * ow[:, c]
        cotw = jnp.concatenate([cotb] * (step // 128), axis=1)
        for t in range(step // 128):
            lsum = lsum + uw[:, t * 128:(t + 1) * 128]
        g_ow[:, c] = jnp.sum(u * cotw, axis=0, keepdims=True)
        dz = cotw * ow[:, c] * (sig * (1.0 + zv * (1.0 - sig)))
        g_tb[:, c] = jnp.sum(dz, axis=0, keepdims=True)
        dzb[:, c] = dz.astype(BF16)
    logits[...] = jnp.sum(lsum.T, axis=0, keepdims=True)

    @pl.loop(0, width // step)
    def _(j):
        c = pl.ds(pl.multiple_of(j * step, step), step)
        dhv = dot(dzb[...], tw[c, :], NT)
        dh[:, c] = dhv
        dy = dhv * x0[:, c].astype(F32)
        g_cb[:, c] = jnp.sum(dy, axis=0, keepdims=True)
        dyb[:, c] = dy.astype(BF16)

    @pl.loop(0, width // step)
    def _(j):
        c = pl.ds(pl.multiple_of(j * step, step), step)
        g_top[c, :] = dot(h[:, c], dzb[...], TN)
        g_cross[c, :] = dot(x0[:, c], dyb[...], TN)

    @pl.loop(0, width // step)
    def _(j):
        c = pl.ds(pl.multiple_of(j * step, step), step)
        dx = dh[:, c] * (y[:, c] + 1.0) + dot(dyb[...], cw[c, :], NT)
        for t in range(step // emb):
            dxhl[j * (step // emb) + t] = split(dx[:, t * emb:(t + 1) * emb])

    sub = lax.broadcasted_iota(I32, (cap, samples), 0)
    for f in range(feats):
        sums = [jnp.zeros((cap, samples), I32)] * groups
        for b in range(bag):
            row = b * feats + f
            code = jnp.broadcast_to(rowcode[row:row + 1, :], (cap, samples)) - sub
            bit = jnp.broadcast_to(rowbit[row:row + 1, :], (cap, samples))
            for w in range(groups):
                sums[w] = sums[w] + jnp.where(code == w * cap, bit, 0)
        for w in range(groups):
            wordst[w, f] = sums[w]

    @pl.loop(0, owners // per)
    def _(g):
        w = g // 2
        total = jnp.zeros((per * cap, 2 * emb), F32)
        for f in range(feats):
            word = wordst[w, f]
            tiles = []
            for i in range(per):
                mask = jnp.left_shift(jnp.int32(15), ((g % 2) * per + i) * 4)
                tiles.append((word & mask).astype(F32).astype(BF16))
            total = total + dot(jnp.concatenate(tiles, axis=0), dxhl[f], NN)
        for i in range(per):
            o = g * per + i
            rows = total[i * cap:(i + 1) * cap]
            slot_grads[o] = (rows[:, :emb] + rows[:, emb:]) * nibble_scale(o)


def local_step(cache, slots, lengths, cot, cw, cb, tw, tb, ow):
    feats, bag, samples = slots.shape
    owners, cap, emb = cache.shape
    width, top = tw.shape
    groups = owners // 8
    vm = pl.BlockSpec(memory_space=pltpu.VMEM)
    out = [
        jax.ShapeDtypeStruct((1, samples), F32),
        jax.ShapeDtypeStruct((width, width), F32),
        jax.ShapeDtypeStruct((width, top), F32),
        jax.ShapeDtypeStruct((1, width), F32),
        jax.ShapeDtypeStruct((1, top), F32),
        jax.ShapeDtypeStruct((1, top), F32),
        jax.ShapeDtypeStruct((owners, cap, emb), F32),
    ]
    keys = feats * bag
    scratch = [
        pltpu.VMEM((groups, feats, samples, cap), I32),
        pltpu.VMEM((groups, feats, cap, samples), I32),
        pltpu.VMEM((samples, keys), I32),
        pltpu.VMEM((samples, keys), I32),
        pltpu.VMEM((keys, samples), I32),
        pltpu.VMEM((keys, samples), I32),
        pltpu.VMEM((feats, samples, 2 * emb), F32),
        pltpu.VMEM((owners * cap, 2 * emb), BF16),
        pltpu.VMEM((samples, width), BF16),
        pltpu.VMEM((samples, width), F32),
        pltpu.VMEM((samples, width), BF16),
        pltpu.VMEM((samples, top), F32),
        pltpu.VMEM((samples, top), BF16),
        pltpu.VMEM((samples, width), BF16),
        pltpu.VMEM((samples, width), F32),
        pltpu.VMEM((feats, samples, 2 * emb), BF16),
    ]
    return pl.pallas_call(
        local_kernel,
        out_shape=out,
        in_specs=[vm] * 9,
        out_specs=[vm] * 7,
        scratch_shapes=scratch,
        compiler_params=pltpu.CompilerParams(vmem_limit_bytes=VMEM_BIG),
        name="local_step",
    )(cache, slots, lengths, cot, cw, cb, tw, tb, ow)

NY = 4


def on_device(table, cross_weight, cross_bias, top_weight, top_bias, out_weight, wanted, slots, lengths, logit_grad):
    emb = table.shape[1]
    cache, served = fetch(wanted[0], table, NY)
    logits, g_cross, g_top, g_cbias, g_tbias, g_out, slot_grads = local_step(
        cache, jnp.transpose(slots, (1, 2, 0)), lengths.T, logit_grad[None], cross_weight, cross_bias[None],
        top_weight, top_bias[None], out_weight[None])
    returned = lax.all_to_all(slot_grads, "shard", split_axis=0, concat_axis=0, tiled=True)
    owner_grad = (
        jnp.zeros(table.shape, jnp.float32).at[served.reshape(-1)].add(returned.reshape(-1, emb))
    )
    table_grad = lax.psum(owner_grad, "dp")
    summed = lax.psum((g_cross, g_top, g_cbias[0], g_tbias[0], g_out[0]), ("dp", "shard"))
    return (logits[0], summed[0], summed[1], summed[2], summed[3], summed[4], table_grad)


def solution(mesh):
    placed = (
        P("shard", None),
        P(),
        P(),
        P(),
        P(),
        P(),
        P(("dp", "shard"), None, None),
        P(("dp", "shard"), None, None),
        P(("dp", "shard"), None),
        P(("dp", "shard")),
    )
    return jax.shard_map(
        on_device,
        mesh=mesh,
        in_specs=placed,
        out_specs=(P(("dp", "shard")), P(), P(), P(), P(), P(), P("shard", None)),
        check_vma=False,
    )
```

time: 661 us -> 523 us (0.79)
  Pallas kernels: 0 us -> 127 us
  other arithmetic: 135 us -> 23.4 us
  local copies, waits for them, and re-layouts: 102 us -> 7.89 us
  waiting for transfers between devices: 288 us -> 263 us
  starting transfers between devices: 24.8 us -> 8.01 us
  matrix products: 14.7 us -> 0 us
    pallas_call x0 -> x2, Pallas kernels: none -> 127 us  [the longest x1 69 us: fetch(): pl.pallas_call(functools.partial(fetch_kernel, n, ny), out_shape=[jax.Sha...]
    scatter-add x1 -> x0, other arithmetic: 97.5 us -> none  [on_device(): jnp.zeros(cache_flat.shape, jnp.float32).at[slots.reshape(-1)]]
    gather x2 -> x0, local copies, waits for them, and re-layouts: 70.3 us -> none  [the longest x1 56.1 us: on_device(): gathered = cache_flat[slots]]
    all_to_all x3 -> x1, waiting for transfers between devices: 81.1 us -> 54.2 us  [on_device(): lax.all_to_all(slot_grads, 'shard', split_axis=0, concat_axis=0, tiled=True)]
    all_to_all x3 -> x1, starting transfers between devices: 24.7 us -> 7.93 us  [on_device(): lax.all_to_all(slot_grads, 'shard', split_axis=0, concat_axis=0, tiled=True)]
    dot_general x8 -> x0, matrix products: 14.7 us -> none  [the longest x1 3.98 us: on_device(): g_top = jnp.dot(hidden.T, dzb, preferred_element_type=jnp.float32)]
    reduce_sum x1 -> x0, other arithmetic: 8.04 us -> none  [on_device(): pooled = jnp.sum(gathered * live[..., None], axis=2)]
    mul x1 -> x0, local copies, waits for them, and re-layouts: 7.35 us -> none  [on_device(): contrib = dx.reshape(samples, feats, 1, emb) * live[..., None]]
  transfers between devices with their start and end apart: 5 -> 3, of which waited for: 5 -> 3; matrix products, arithmetic and copies ran while one was open for 8% -> 4% of each run, Pallas kernels for 0% -> 0%
where the time goes in v1:
time: 523 us; the launch traced here: 522 us
  waiting for transfers between devices  263 us (50%)
  Pallas kernels  127 us (24%)
  blocking collectives  77.9 us (15%)
  other arithmetic  23.4 us (4%)
  between operations  14.1 us (3%)
  starting transfers between devices  8.01 us (2%)
  local copies, waits for them, and re-layouts  7.89 us (2%)
    psum x1, waiting for transfers between devices, on_device(): lax.psum((g_cross, g_top, g_cbias[0], g_tbias[0], g_out[0]), ('dp', 'shar...  140 us
    psum x1, blocking collectives, on_device(): lax.psum((g_cross, g_top, g_cbias[0], g_tbias[0], g_out[0]), ('dp', 'shar...  77.9 us
    pallas_call x1, Pallas kernels, fetch(): pl.pallas_call(functools.partial(fetch_kernel, n, ny), out_shape=[jax.Sha...  69 us
    psum x1, waiting for transfers between devices, on_device(): table_grad = lax.psum(owner_grad, 'dp')  68.7 us
    pallas_call x1, Pallas kernels, local_step(): pl.pallas_call(local_kernel, out_shape=out, in_specs=[vm] * 9, out_specs=...  58.1 us
    all_to_all x1, waiting for transfers between devices, on_device(): lax.all_to_all(slot_grads, 'shard', split_axis=0, concat_axis=0, tiled=True)  54.2 us
    scatter-add x1, other arithmetic, on_device(): jnp.zeros(table.shape, jnp.float32).at[served.reshape(-1)]  23.3 us
  transfers between devices with their start and end apart: 3, of which 3 were waited for; matrix products, arithmetic and copies ran while one was open for 4% of the time, Pallas kernels for 0%

profile of v1, /device:TPU:1, one launch (start us, length us, event | category | flops | bytes accessed | tf_op | source)
XLA Modules:
  0.0 521.9 jit_solution(10789992603861787785)
XLA Ops:
  7.2 69.0 %fetch_rows.1 = (f32[32,128,128]{2,1,0:T(8,128)}, s32[32,1,128]{2,1,0:T(1,128)}) custom-call(s32[32,1,128]{2,1,0:T(1,128)} %bitcast.17, f32[2048,128]{1,0:T(8,128)} %table.1), custom_call_target="tpu_custom_call" | custom-call | tf_op jit(solution)/shard_map/fetch_rows/pallas_call | solution.py:99
  76.1 58.1 %local_step.1 = (f32[1,512]{1,0:T(1,128)}, f32[1024,1024]{1,0:T(8,128)}, f32[1024,512]{1,0:T(8,128)}, f32[1,1024]{1,0:T(1,128)}, f32[1,512]{1,0:T(1,128)}, /*index=5*/f32[1,512]{1,0:T(1,128)}, f32[32,128,128]{2,1,0:T(8,128)}) custom-call(f32[32,128,128]{2,1,0:T(8,128)} %get-tuple-element.16.cache, s32[8,4,512]{2,1,0:T(4,128)} %bitcast.16, ...), custom_call_target="tpu_custom_call" | custom-call | tf_op jit(solution)/shard_map/local_step/pallas_call | solution.py:324
  134.3 7.9 %all-to-all-start = ((f32[32,128,128]{2,1,0:T(8,128)}), f32[32,128,128]{2,1,0:T(8,128)S(1)}, u32[]{:S(2)}, u32[]{:S(2)}) async-start(f32[32,128,128]{2,1,0:T(8,128)} %get-tuple-element.24), calls=%async_computation | async-start | bytes 4194304 | tf_op jit(solution)/shard_map/all_to_all | solution.py:343
  142.2 0.0 all-reduce.7.cloned.1.call-start
  142.3 0.0 copy-start.2
  142.3 0.7 all-reduce.7.cloned.1.call-update
  143.0 0.0 copy-start.3
  143.0 0.0 copy-start.4
  143.0 0.0 copy-start.5
  143.0 0.0 all-reduce.5.cloned.1.call-start
  143.0 0.0 copy-done.2
  143.1 54.2 %all-to-all-done = f32[32,128,128]{2,1,0:T(8,128)S(1)} async-done(((f32[32,128,128]{2,1,0:T(8,128)}), f32[32,128,128]{2,1,0:T(8,128)S(1)}, u32[]{:S(2)}, u32[]{:S(2)}) %all-to-all-start) | async-done | bytes 2097184 | tf_op jit(solution)/shard_map/all_to_all | solution.py:343
  197.3 23.3 %scatter_custom_fusion = f32[2048,128]{1,0:T(8,128)} fusion(s32[4096]{0:T(1024)S(1)} %bitcast.19, f32[4096,128]{1,0:T(8,128)S(1)} %bitcast.15, f32[]{:T(128)} %constant.0.clone.1), kind=kCustom, calls=%fused_computation.1 | custom fusion | flops 524288 | bytes 1048580 | tf_op jit(solution)/shard_map/scatter-add | solution.py:345
  220.7 0.0 all-reduce.5.cloned.1.call-update
  220.7 0.0 copy-done.3
  220.7 0.0 copy-done.4
  220.7 0.0 copy-done.5
  220.7 77.9 %all-reduce = (f32[1024]{0:T(1024)}, f32[512]{0:T(512)}, f32[512]{0:T(512)}) all-reduce(f32[1024]{0:T(1024)S(1)} %bitcast.21, f32[512]{0:T(512)S(1)} %bitcast.25, f32[512]{0:T(512)S(1)} %bitcast.26), channel_id=1, replica_groups=mesh['dp'=8,'shard'=32] {'dp','shard'}, use_global_device_ids=true, to_apply=%region_2.0 | all-reduce | flops 2048 | bytes 16384 | tf_op jit(solution)/shard_map/psum | solution.py:348
  298.6 139.9 %all-reduce.7.cloned.1.call-done = (f32[1024,1024]{1,0:T(8,128)}, f32[1024,512]{1,0:T(8,128)}) async-done(((f32[1024,1024]{1,0:T(8,128)}, f32[1024,512]{1,0:T(8,128)}), (f32[1024,1024]{1,0:T(8,128)}, f32[1024,512]{1,0:T(8,128)})) %all-reduce.7.cloned.1.call-update) | async-done | bytes 6291472 | tf_op jit(solution)/shard_map/psum | solution.py:348
  438.5 68.7 %all-reduce.5.cloned.1.call-done = f32[2048,128]{1,0:T(8,128)} async-done(((f32[2048,128]{1,0:T(8,128)}), f32[2048,128]{1,0:T(8,128)}) %all-reduce.5.cloned.1.call-update) | async-done | bytes 1048592 | tf_op jit(solution)/shard_map/psum | solution.py:347
  507.2 0.0 copy-start
  507.2 4.9 copy.20
  512.1 0.0 copy-done
  512.1 0.0 copy-start.1
  512.1 1.3 copy.21
  513.4 0.6 copy-done.1
  514.1 1.0 copy.22
  (1 shorter events, 0.0 us)
Async XLA Ops:
  134.3 63.0 %all-to-all-start = ((f32[32,128,128]{2,1,0:T(8,128)}), f32[32,128,128]{2,1,0:T(8,128)S(1)}, u32[]{:S(2)}, u32[]{:S(2)}) async-start(f32[32,128,128]{2,1,0:T(8,128)} %get-tuple-element.24), calls=%async_computation | async-start | bytes 4194304 | tf_op jit(solution)/shard_map/all_to_all | solution.py:343
  142.2 296.3 %all-reduce.7.cloned.1.call-start = ((), (), s32[]{:S(2)}) async-start(), calls=%async_computation.2 | async-start | bytes 12582912 | tf_op jit(solution)/shard_map/psum | solution.py:348
  142.3 0.8 copy-start.2
  143.0 77.7 %copy-start.3 = (f32[1,1024]{1,0:T(1,128)S(1)}, f32[1,1024]{1,0:T(1,128)}, u32[]{:S(2)}) copy-start(f32[1,1024]{1,0:T(1,128)} %get-tuple-element.20) | copy-start | bytes 12292
  143.0 77.7 %copy-start.4 = (f32[1,512]{1,0:T(1,128)S(1)}, f32[1,512]{1,0:T(1,128)}, u32[]{:S(2)}) copy-start(f32[1,512]{1,0:T(1,128)} %get-tuple-element.21) | copy-start | bytes 6148
  143.0 77.7 %copy-start.5 = (f32[1,512]{1,0:T(1,128)S(1)}, f32[1,512]{1,0:T(1,128)}, u32[]{:S(2)}) copy-start(f32[1,512]{1,0:T(1,128)} %get-tuple-element.22) | copy-start | bytes 6148
  143.0 364.2 %all-reduce.5.cloned.1.call-start = ((), (), s32[]{:S(2)}) async-start(), calls=%async_computation.1 | async-start | bytes 2097152 | tf_op jit(solution)/shard_map/psum | solution.py:347
  507.2 4.9 copy-start
  512.1 2.0 copy-start.1
Sparse Core Ops, SparseCore 0:
  149.2 289.2 all-reduce.6
  441.5 65.5 all-reduce.4

commit v2 on v0

v2 whole, which is shorter than its diff:
```python
import functools
import jax
import jax.numpy as jnp
from jax import lax
from jax.experimental import pallas as pl
from jax.experimental.pallas import tpu as pltpu
from jax.sharding import PartitionSpec as P

VMEM_BIG = 60 * 1024 * 1024
F32, BF16, I32 = jnp.float32, jnp.bfloat16, jnp.int32


def dot(a, b, dims):
    return lax.dot_general(a, b, (dims, ((), ())), preferred_element_type=F32)


NN = ((1,), (0,))
NT = ((1,), (1,))
TN = ((0,), (0,))


def split(x):
    hi = x.astype(BF16)
    lo = (x - hi.astype(F32)).astype(BF16)
    return jnp.concatenate([hi, lo], axis=1)


def nibble_scale(o):
    k = o % 8
    s = jnp.where((k & 1) == 1, F32(2.0**-4), F32(1.0))
    s = s * jnp.where((k & 2) == 2, F32(2.0**-8), F32(1.0))
    return s * jnp.where((k & 4) == 4, F32(2.0**-16), F32(1.0))


def key_codes(slots, lengths, b):
    slot = slots[:, b, :]
    owner = slot >> 7
    code = jnp.where(lengths[...] > b, (slot & 127) + ((owner >> 3) << 7), -1)
    return code, jnp.left_shift(jnp.ones_like(owner), (owner & 7) << 2)


def local_kernel(cache, slots, lengths, cot, cw, cb, tw, tb, ow,
                 logits, dense, small, slot_grads,
                 words, wordst, colcode, colbit, rowcode, rowbit, acc, chl, x0, y, h, z, dzb, dyb, dh, dxhl):
    feats, bag, samples = slots.shape
    owners, cap, emb = cache.shape
    width, top = tw.shape
    groups = words.shape[0]

    for b in range(bag):
        code, bit = key_codes(slots, lengths, b)
        rowcode[pl.ds(b * feats, feats), :] = code
        rowbit[pl.ds(b * feats, feats), :] = bit
    colcode[...] = rowcode[...].T
    colbit[...] = rowbit[...].T

    lane = lax.broadcasted_iota(I32, (samples, cap), 1)
    for f in range(feats):
        sums = [jnp.zeros((samples, cap), I32)] * groups
        for b in range(bag):
            col = b * feats + f
            code = jnp.broadcast_to(colcode[:, col:col + 1], (samples, cap)) - lane
            bit = jnp.broadcast_to(colbit[:, col:col + 1], (samples, cap))
            for w in range(groups):
                sums[w] = sums[w] + jnp.where(code == w * cap, bit, 0)
        for w in range(groups):
            words[w, f] = sums[w]

    for o in range(owners):
        scale = 2.0 ** -(4 * (o % 8))
        chl[pl.ds(o * cap, cap), :] = split(cache[o] * scale)

    per = 4

    @pl.loop(0, owners // per)
    def _(g):
        w = g // 2
        rhs = chl[pl.ds(g * per * cap, per * cap), :]

        @pl.loop(0, feats)
        def _(f):
            word = words[w, f]
            tiles = []
            for i in range(per):
                mask = jnp.left_shift(jnp.int32(15), ((g % 2) * per + i) * 4)
                tiles.append((word & mask).astype(F32).astype(BF16))
            part = dot(jnp.concatenate(tiles, axis=1), rhs, NN)

            @pl.when(g == 0)
            def _():
                acc[f] = part

            @pl.when(g > 0)
            def _():
                acc[f] += part

    for f in range(feats):
        x0[:, f * emb:(f + 1) * emb] = (acc[f, :, :emb] + acc[f, :, emb:]).astype(BF16)

    step = 256

    def put_dense(j, at, val):
        n = step // 8
        for t in range(val.shape[1] // 128):
            dense[pl.ds(j * n, n), at + t] = val[:, t * 128:(t + 1) * 128].reshape(n, 8, 128)

    def put_small(at, row, vec):
        for t in range(step // 128):
            small[pl.ds(at + row + t, 1), :] = vec[:, t * 128:(t + 1) * 128]

    @pl.loop(0, width // step)
    def _(j):
        c = pl.ds(pl.multiple_of(j * step, step), step)
        yv = dot(x0[...], cw[:, c], NN) + cb[:, c]
        y[:, c] = yv
        xf = x0[:, c].astype(F32)
        h[:, c] = (xf * yv + xf).astype(BF16)

    cotb = jnp.broadcast_to(cot[...], (128, samples)).T
    lsum = jnp.zeros((samples, 128), F32)
    for j in range(top // step):
        c = pl.ds(j * step, step)
        zv = dot(h[...], tw[:, c], NN) + tb[:, c]
        sig = jax.nn.sigmoid(zv)
        u = zv * sig
        uw = u * ow[:, c]
        cotw = jnp.concatenate([cotb] * (step // 128), axis=1)
        for t in range(step // 128):
            lsum = lsum + uw[:, t * 128:(t + 1) * 128]
        put_small((width + top) // 128, j * (step // 128), jnp.sum(u * cotw, axis=0, keepdims=True))
        dz = cotw * ow[:, c] * (sig * (1.0 + zv * (1.0 - sig)))
        put_small(width // 128, j * (step // 128), jnp.sum(dz, axis=0, keepdims=True))
        dzb[:, c] = dz.astype(BF16)
    logits[...] = jnp.sum(lsum.T, axis=0, keepdims=True)

    @pl.loop(0, width // step)
    def _(j):
        c = pl.ds(pl.multiple_of(j * step, step), step)
        dhv = dot(dzb[...], tw[c, :], NT)
        dh[:, c] = dhv
        dy = dhv * x0[:, c].astype(F32)
        put_small(0, j * (step // 128), jnp.sum(dy, axis=0, keepdims=True))
        dyb[:, c] = dy.astype(BF16)

    @pl.loop(0, width // step)
    def _(j):
        c = pl.ds(pl.multiple_of(j * step, step), step)
        put_dense(j, width // 128, dot(h[:, c], dzb[...], TN))
        put_dense(j, 0, dot(x0[:, c], dyb[...], TN))

    @pl.loop(0, width // step)
    def _(j):
        c = pl.ds(pl.multiple_of(j * step, step), step)
        dx = dh[:, c] * (y[:, c] + 1.0) + dot(dyb[...], cw[c, :], NT)
        for t in range(step // emb):
            dxhl[j * (step // emb) + t] = split(dx[:, t * emb:(t + 1) * emb])

    sub = lax.broadcasted_iota(I32, (cap, samples), 0)
    for f in range(feats):
        sums = [jnp.zeros((cap, samples), I32)] * groups
        for b in range(bag):
            row = b * feats + f
            code = jnp.broadcast_to(rowcode[row:row + 1, :], (cap, samples)) - sub
            bit = jnp.broadcast_to(rowbit[row:row + 1, :], (cap, samples))
            for w in range(groups):
                sums[w] = sums[w] + jnp.where(code == w * cap, bit, 0)
        for w in range(groups):
            wordst[w, f] = sums[w]

    @pl.loop(0, owners // per)
    def _(g):
        w = g // 2
        total = jnp.zeros((per * cap, 2 * emb), F32)
        for f in range(feats):
            word = wordst[w, f]
            tiles = []
            for i in range(per):
                mask = jnp.left_shift(jnp.int32(15), ((g % 2) * per + i) * 4)
                tiles.append((word & mask).astype(F32).astype(BF16))
            total = total + dot(jnp.concatenate(tiles, axis=0), dxhl[f], NN)
        for i in range(per):
            o = g * per + i
            rows = total[i * cap:(i + 1) * cap]
            slot_grads[o] = (rows[:, :emb] + rows[:, emb:]) * nibble_scale(o)


def local_step(cache, slots, lengths, cot, cw, cb, tw, tb, ow):
    feats, bag, samples = slots.shape
    owners, cap, emb = cache.shape
    width, top = tw.shape
    groups = owners // 8
    vm = pl.BlockSpec(memory_space=pltpu.VMEM)
    out = [
        jax.ShapeDtypeStruct((1, samples), F32),
        jax.ShapeDtypeStruct((width // 8, (width + top) // 128, 8, 128), F32),
        jax.ShapeDtypeStruct(((width + 2 * top) // 128, 128), F32),
        jax.ShapeDtypeStruct((owners, cap, emb), F32),
    ]
    keys = feats * bag
    scratch = [
        pltpu.VMEM((groups, feats, samples, cap), I32),
        pltpu.VMEM((groups, feats, cap, samples), I32),
        pltpu.VMEM((samples, keys), I32),
        pltpu.VMEM((samples, keys), I32),
        pltpu.VMEM((keys, samples), I32),
        pltpu.VMEM((keys, samples), I32),
        pltpu.VMEM((feats, samples, 2 * emb), F32),
        pltpu.VMEM((owners * cap, 2 * emb), BF16),
        pltpu.VMEM((samples, width), BF16),
        pltpu.VMEM((samples, width), F32),
        pltpu.VMEM((samples, width), BF16),
        pltpu.VMEM((samples, top), F32),
        pltpu.VMEM((samples, top), BF16),
        pltpu.VMEM((samples, width), BF16),
        pltpu.VMEM((samples, width), F32),
        pltpu.VMEM((feats, samples, 2 * emb), BF16),
    ]
    return pl.pallas_call(
        local_kernel,
        out_shape=out,
        in_specs=[vm] * 9,
        out_specs=[vm] * 4,
        scratch_shapes=scratch,
        compiler_params=pltpu.CompilerParams(vmem_limit_bytes=VMEM_BIG),
        name="local_step",
    )(cache, slots, lengths, cot, cw, cb, tw, tb, ow)


def peer_of(k, me, ny, nz):
    j = k // ny
    dz = nz // 2 + (j // 2 + j % 2) * (1 - 2 * (j % 2))
    dy = (k + 1) % ny
    z = (me // ny + dz + nz) % nz
    y = (me % ny + dy) % ny
    return z * ny + y


def fetch_kernel(n, ny, wanted, table, cache, ids_in, ids_sm, sendbuf,
                 id_send, id_recv, row_send, row_recv, sm_sem):
    nz = n // ny
    cap = wanted.shape[2]
    me = lax.axis_index("shard")
    barrier = pltpu.get_barrier_semaphore()

    @pl.loop(0, n - 1)
    def _(k):
        pl.semaphore_signal(barrier, inc=1, device_id={"shard": peer_of(k, me, ny, nz)})

    pl.semaphore_wait(barrier, n - 1)

    def id_copy(p):
        return pltpu.make_async_remote_copy(
            src_ref=wanted.at[p], dst_ref=ids_in.at[me], send_sem=id_send.at[p],
            recv_sem=id_recv.at[me], device_id={"shard": p})

    def id_arrival(p):
        return pltpu.make_async_remote_copy(
            src_ref=wanted.at[p], dst_ref=ids_in.at[p], send_sem=id_send.at[p],
            recv_sem=id_recv.at[p], device_id={"shard": p})

    def row_copy(p):
        return pltpu.make_async_remote_copy(
            src_ref=sendbuf.at[p], dst_ref=cache.at[me], send_sem=row_send.at[p],
            recv_sem=row_recv.at[me], device_id={"shard": p})

    def row_arrival(p):
        return pltpu.make_async_remote_copy(
            src_ref=sendbuf.at[p], dst_ref=cache.at[p], send_sem=row_send.at[p],
            recv_sem=row_recv.at[p], device_id={"shard": p})

    @pl.loop(0, n - 1)
    def _(k):
        id_copy(peer_of(k, me, ny, nz)).start()

    ids_in[me] = wanted[me]

    @pl.loop(0, n - 1)
    def _(k):
        id_arrival(peer_of(k, me, ny, nz)).wait_recv()

    to_smem = pltpu.make_async_copy(ids_in, ids_sm, sm_sem)
    to_smem.start()
    to_smem.wait()

    def serve(p, out):
        @pl.loop(0, cap // 16)
        def _(t):
            for i in range(16):
                row = t * 16 + i
                out[p, pl.ds(row, 1), :] = table[pl.ds(ids_sm[p, 0, row], 1), :]

    @pl.loop(0, n - 1)
    def _(k):
        p = peer_of(k, me, ny, nz)
        serve(p, sendbuf)
        row_copy(p).start()

    serve(me, cache)

    @pl.loop(0, n - 1)
    def _(k):
        p = peer_of(k, me, ny, nz)
        row_arrival(p).wait_recv()

    @pl.loop(0, n - 1)
    def _(k):
        p = peer_of(k, me, ny, nz)
        id_copy(p).wait_send()
        row_copy(p).wait_send()


def fetch(wanted, table, ny):
    n, cap = wanted.shape
    emb = table.shape[1]
    vm = pl.BlockSpec(memory_space=pltpu.VMEM)
    cache, served = pl.pallas_call(
        functools.partial(fetch_kernel, n, ny),
        out_shape=[
            jax.ShapeDtypeStruct((n, cap, emb), jnp.float32),
            jax.ShapeDtypeStruct((n, 1, cap), jnp.int32),
        ],
        in_specs=[vm, vm],
        out_specs=[vm, vm],
        scratch_shapes=[
            pltpu.SMEM((n, 1, cap), jnp.int32),
            pltpu.VMEM((n, cap, emb), jnp.float32),
            pltpu.SemaphoreType.DMA((n,)),
            pltpu.SemaphoreType.DMA((n,)),
            pltpu.SemaphoreType.DMA((n,)),
            pltpu.SemaphoreType.DMA((n,)),
            pltpu.SemaphoreType.DMA,
        ],
        compiler_params=pltpu.CompilerParams(
            collective_id=0, has_side_effects=True, vmem_limit_bytes=VMEM_BIG),
        name="fetch_rows",
    )(wanted.reshape(n, 1, cap), table)
    return cache, served


def add_tiles(out, parts, count, chunk):
    chunk = min(chunk, count)

    @pl.loop(0, count // chunk)
    def _(t):
        w = pl.ds(t * chunk, chunk)
        total = parts[0][w]
        for p in parts[1:]:
            total = total + p[w]
        out[w] = total


class Group:
    def __init__(self, size, me, address):
        self.size, self.me, self.address = size, me, address

    def others(self):
        return [(d, (self.me + d) % self.size) for d in range(1, self.size)]


def spread(group, src, dst, send, recv):
    copies = []
    for d, j in group.others():
        cp = pltpu.make_async_remote_copy(
            src_ref=src(j), dst_ref=dst(group.me), send_sem=send.at[d],
            recv_sem=recv.at[group.me], device_id=group.address(j))
        cp.start()
        copies.append(cp)
    return copies


def gather_wait(group, src, dst, send, recv):
    for d, j in group.others():
        pltpu.make_async_remote_copy(
            src_ref=src(j), dst_ref=dst(j), send_sem=send.at[d],
            recv_sem=recv.at[j], device_id=group.address(j)).wait_recv()


def reduce_kernel(nx, ny, nz, slot_grads, served, dense, small,
                  table_out, dense_out, small_out,
                  back, tsum, rt1, rt2, r1, r2, r3, r4, b, c3,
                  s_core, s_x, s_y, s_z, sm1, sm2, sm3,
                  g_send, g_recv, core_send, core_recv, st_send, st_recv, z_send, z_recv, sm_send, sm_recv):
    n = ny * nz
    cap = served.shape[2]
    emb = slot_grads.shape[2]
    rows = tsum.shape[0]
    dp, me = lax.axis_index("dp"), lax.axis_index("shard")
    x, core, z, y = dp // 2, dp % 2, me // ny, me % ny
    gx = Group(nx, x, lambda j: {"dp": j * 2 + core})
    gy = Group(ny, y, lambda j: {"shard": z * ny + j})
    gz = Group(nz, z, lambda j: {"shard": j * ny + y})
    gc = Group(2, core, lambda j: {"dp": x * 2 + j})

    barrier = pltpu.get_barrier_semaphore()

    @pl.loop(0, n - 1)
    def _(k):
        pl.semaphore_signal(barrier, inc=1, device_id={"shard": peer_of(k, me, ny, nz)})

    for grp in (gx, gc):
        for _, j in grp.others():
            pl.semaphore_signal(barrier, inc=1, device_id=grp.address(j))
    pl.semaphore_wait(barrier, n - 1 + nx - 1 + 1)

    pending = []
    tiles = dense.shape[0]
    half = tiles // 2
    quarter = half // 2
    order = [(gx, gy), (gy, gx)]

    mine = lambda h: dense.at[pl.ds(core * half + h * quarter, quarter)]
    theirs = lambda h: dense.at[pl.ds((1 - core) * half + h * quarter, quarter)]
    for h in range(2):
        pending += spread(gc, lambda j: theirs(h), lambda i: r1.at[h], core_send.at[h], core_recv.at[h])
    s_core[core] = small[...]
    pending += spread(gc, lambda j: small, lambda i: s_core.at[i], sm_send.at[0], sm_recv.at[0])

    def grad_copy(p):
        return pltpu.make_async_remote_copy(
            src_ref=slot_grads.at[p], dst_ref=back.at[me], send_sem=g_send.at[p],
            recv_sem=g_recv.at[me], device_id={"shard": p})

    def grad_arrival(p):
        return pltpu.make_async_remote_copy(
            src_ref=slot_grads.at[p], dst_ref=back.at[p], send_sem=g_send.at[p],
            recv_sem=g_recv.at[p], device_id={"shard": p})

    @pl.loop(0, n - 1)
    def _(k):
        grad_copy(peer_of(k, me, ny, nz)).start()

    back[me] = slot_grads[me]

    piece = [quarter // order[h][0].size for h in range(2)]
    sub = [piece[h] // order[h][1].size for h in range(2)]
    unit = sub[0] // nz

    def small_sum(slots, out):
        total = slots[0]
        for i in range(1, slots.shape[0]):
            total = total + slots[i]
        out[...] = total

    for h in range(2):
        grp = order[h][0]
        gather_wait(gc, lambda j: theirs(h), lambda i: r1.at[h], core_send.at[h], core_recv.at[h])
        add_tiles(r1.at[h], [r1.at[h], mine(h)], quarter, 32)
        src = lambda j: r1.at[h, pl.ds(j * piece[h], piece[h])]
        pending += spread(grp, src, lambda i: r2[h].at[i], st_send.at[0, h], st_recv.at[0, h])
    gather_wait(gc, lambda j: small, lambda i: s_core.at[i], sm_send.at[0], sm_recv.at[0])
    small_sum(s_core, sm1)
    s_x[x] = sm1[...]
    pending += spread(gx, lambda j: sm1, lambda i: s_x.at[i], sm_send.at[1], sm_recv.at[1])

    for h in range(2):
        grp, nxt = order[h]
        src = lambda j: r1.at[h, pl.ds(j * piece[h], piece[h])]
        gather_wait(grp, src, lambda i: r2[h].at[i], st_send.at[0, h], st_recv.at[0, h])
        add_tiles(b[h], [src(grp.me)] + [r2[h].at[j] for _, j in grp.others()], piece[h], 24)
        src2 = lambda j: b[h].at[pl.ds(j * sub[h], sub[h])]
        pending += spread(nxt, src2, lambda i: r3[h].at[i], st_send.at[1, h], st_recv.at[1, h])
    gather_wait(gx, lambda j: sm1, lambda i: s_x.at[i], sm_send.at[1], sm_recv.at[1])
    small_sum(s_x, sm2)
    s_y[y] = sm2[...]
    pending += spread(gy, lambda j: sm2, lambda i: s_y.at[i], sm_send.at[2], sm_recv.at[2])

    for h in range(2):
        nxt = order[h][1]
        src2 = lambda j: b[h].at[pl.ds(j * sub[h], sub[h])]
        gather_wait(nxt, src2, lambda i: r3[h].at[i], st_send.at[1, h], st_recv.at[1, h])
        add_tiles(c3.at[h], [src2(nxt.me)] + [r3[h].at[j] for _, j in nxt.others()], sub[h], 24)
        src3 = lambda j: c3.at[h, pl.ds(j * unit, unit)]
        pending += spread(gz, src3, lambda i: r4.at[h, i], z_send.at[0, h], z_recv.at[0, h])
    gather_wait(gy, lambda j: sm2, lambda i: s_y.at[i], sm_send.at[2], sm_recv.at[2])
    small_sum(s_y, sm3)
    s_z[z] = sm3[...]
    pending += spread(gz, lambda j: sm3, lambda i: s_z.at[i], sm_send.at[3], sm_recv.at[3])

    def at1(h, a):
        return core * half + h * quarter + a * piece[h]

    def at2(h, a, bb):
        return at1(h, a) + bb * sub[h]

    def at3(h, zz):
        return at2(h, order[h][0].me, order[h][1].me) + zz * unit

    for h in range(2):
        src3 = lambda j: c3.at[h, pl.ds(j * unit, unit)]
        gather_wait(gz, src3, lambda i: r4.at[h, i], z_send.at[0, h], z_recv.at[0, h])
        here = lambda i: dense_out.at[pl.ds(at3(h, i), unit)]
        add_tiles(here(z), [src3(z)] + [r4.at[h, j] for _, j in gz.others()], unit, unit)
        pending += spread(gz, lambda j: here(z), here, z_send.at[1, h], z_recv.at[1, h])
    gather_wait(gz, lambda j: sm3, lambda i: s_z.at[i], sm_send.at[3], sm_recv.at[3])
    small_sum(s_z, small_out)

    def owner_sum(j):
        zp = (z + nz // 2 - (j // 2 + j % 2) * (1 - 2 * (j % 2)) + nz) % nz
        first = zp * ny

        @pl.loop(0, ny)
        def _(i):
            p = first + i

            @pl.when(p != me)
            def _():
                grad_arrival(p).wait_recv()

        rhs = jnp.concatenate([split(back[first + i]) for i in range(ny)], axis=0)
        ids = jnp.concatenate([served[first + i] for i in range(ny)], axis=1)
        step = 256

        @pl.loop(0, rows // step)
        def _(t):
            at = t * step
            row = lax.broadcasted_iota(I32, (step, ny * cap), 0) + at
            hot = jnp.where(row == ids, F32(1), F32(0)).astype(BF16)
            part = dot(hot, rhs, NN)
            part = part[:, :emb] + part[:, emb:]
            w = pl.ds(pl.multiple_of(at, step), step)
            tsum[w] = jnp.where(j == 0, part, tsum[w] + part)

    @pl.loop(0, nz)
    def _(j):
        owner_sum(j)

    for h in range(2):
        nxt = order[h][1]
        here = lambda i: dense_out.at[pl.ds(at3(h, i), unit)]
        gather_wait(gz, lambda j: here(z), here, z_send.at[1, h], z_recv.at[1, h])
        here2 = lambda i: dense_out.at[pl.ds(at2(h, order[h][0].me, i), sub[h])]
        pending += spread(nxt, lambda j: here2(nxt.me), here2, st_send.at[2, h], st_recv.at[2, h])

    thalf = rows // 2
    tq = thalf // nx
    tw = lambda c: tsum.at[pl.ds(pl.multiple_of(c * thalf, thalf), thalf)]
    pending += spread(gc, lambda j: tw(j), lambda i: rt1, core_send.at[2], core_recv.at[2])

    for h in range(2):
        grp, nxt = order[h]
        here2 = lambda i: dense_out.at[pl.ds(at2(h, grp.me, i), sub[h])]
        gather_wait(nxt, lambda j: here2(nxt.me), here2, st_send.at[2, h], st_recv.at[2, h])
        here1 = lambda i: dense_out.at[pl.ds(at1(h, i), piece[h])]
        pending += spread(grp, lambda j: here1(grp.me), here1, st_send.at[3, h], st_recv.at[3, h])

    gather_wait(gc, lambda j: tw(j), lambda i: rt1, core_send.at[2], core_recv.at[2])
    rt1[...] = rt1[...] + tsum[pl.ds(pl.multiple_of(core * thalf, thalf), thalf)]
    tsrc = lambda j: rt1.at[pl.ds(pl.multiple_of(j * tq, tq), tq)]
    pending += spread(gx, tsrc, lambda i: rt2.at[i], st_send.at[4, 0], st_recv.at[4, 0])

    for h in range(2):
        grp = order[h][0]
        here1 = lambda i: dense_out.at[pl.ds(at1(h, i), piece[h])]
        gather_wait(grp, lambda j: here1(grp.me), here1, st_send.at[3, h], st_recv.at[3, h])
        part = lambda i: dense_out.at[pl.ds(i * half + h * quarter, quarter)]
        pending += spread(gc, lambda j: part(core), part, core_send.at[3 + h], core_recv.at[3 + h])

    gather_wait(gx, tsrc, lambda i: rt2.at[i], st_send.at[4, 0], st_recv.at[4, 0])
    tplace = lambda c, i: table_out.at[pl.ds(pl.multiple_of(c * thalf + i * tq, tq), tq)]
    total = rt1[pl.ds(pl.multiple_of(x * tq, tq), tq)]
    for _, j in gx.others():
        total = total + rt2[j]
    table_out[pl.ds(pl.multiple_of(core * thalf + x * tq, tq), tq)] = total
    there = lambda i: tplace(core, i)
    pending += spread(gx, lambda j: there(x), there, st_send.at[4, 1], st_recv.at[4, 1])
    gather_wait(gx, lambda j: there(x), there, st_send.at[4, 1], st_recv.at[4, 1])
    tside = lambda i: table_out.at[pl.ds(pl.multiple_of(i * thalf, thalf), thalf)]
    pending += spread(gc, lambda j: tside(core), tside, core_send.at[5], core_recv.at[5])

    for h in range(2):
        part = lambda i: dense_out.at[pl.ds(i * half + h * quarter, quarter)]
        gather_wait(gc, lambda j: part(core), part, core_send.at[3 + h], core_recv.at[3 + h])
    gather_wait(gc, lambda j: tside(core), tside, core_send.at[5], core_recv.at[5])

    for cp in pending:
        cp.wait_send()

    @pl.loop(0, n - 1)
    def _(k):
        grad_copy(peer_of(k, me, ny, nz)).wait_send()


def reduce_all(slot_grads, served, dense, small, nx, ny, nz, rows):
    n, cap, emb = slot_grads.shape
    tiles = dense.shape[0]
    quarter = tiles // 4
    vm = pl.BlockSpec(memory_space=pltpu.VMEM)
    t = lambda *lead: pltpu.VMEM((*lead, 8, 128), F32)
    ns = (nx, ny)
    sizes = [(nx, ny), (ny, nx)]
    piece = [quarter // a for a, _ in sizes]
    sub = quarter // (nx * ny)
    sm = small.shape
    top = max(nx, ny)
    dma = lambda *s: pltpu.SemaphoreType.DMA(s)

    def body(*refs):
        ins, outs, rest = refs[:4], refs[4:7], refs[7:]
        back, tsum, rt1, rt2, r1, r2a, r2b, r3a, r3b, r4, ba, bb, c3 = rest[:13]
        reduce_kernel(nx, ny, nz, *ins, *outs, back, tsum, rt1, rt2, r1, (r2a, r2b), (r3a, r3b), r4, (ba, bb), c3, *rest[13:])

    return pl.pallas_call(
        body,
        out_shape=[
            jax.ShapeDtypeStruct((rows, emb), F32),
            jax.ShapeDtypeStruct(dense.shape, F32),
            jax.ShapeDtypeStruct(sm, F32),
        ],
        in_specs=[vm] * 4,
        out_specs=[vm] * 3,
        scratch_shapes=[
            pltpu.VMEM((n, cap, emb), F32),
            pltpu.VMEM((rows, emb), F32),
            pltpu.VMEM((rows // 2, emb), F32),
            pltpu.VMEM((nx, rows // 2 // nx, emb), F32),
            t(2, quarter),
            t(nx, piece[0]), t(ny, piece[1]),
            t(ny, sub), t(nx, sub),
            t(2, nz, sub // nz),
            t(piece[0]), t(piece[1]),
            t(2, sub),
            pltpu.VMEM((2, *sm), F32), pltpu.VMEM((nx, *sm), F32), pltpu.VMEM((ny, *sm), F32), pltpu.VMEM((nz, *sm), F32),
            pltpu.VMEM(sm, F32), pltpu.VMEM(sm, F32), pltpu.VMEM(sm, F32),
            dma(n), dma(n),
            dma(6, 2), dma(6, 2),
            dma(5, 2, top), dma(5, 2, top),
            dma(2, 2, nz), dma(2, 2, nz),
            dma(4, max(nz, top)), dma(4, max(nz, top)),
        ],
        compiler_params=pltpu.CompilerParams(
            collective_id=1, has_side_effects=True, vmem_limit_bytes=VMEM_BIG),
        name="reduce_all",
    )(slot_grads, served, dense, small)


NX, NY = 4, 4


def on_device(table, cross_weight, cross_bias, top_weight, top_bias, out_weight, wanted, slots, lengths, logit_grad):
    width, top = top_weight.shape
    n = wanted.shape[1]
    cache, served = fetch(wanted[0], table, NY)
    logits, dense, small, slot_grads = local_step(
        cache, jnp.transpose(slots, (1, 2, 0)), lengths.T, logit_grad[None], cross_weight, cross_bias[None],
        top_weight, top_bias[None], out_weight[None])
    table_grad, summed, vecs = reduce_all(
        slot_grads, served, dense.reshape(-1, 8, 128), small, NX, NY, n // NY, table.shape[0])
    tiles = summed.reshape(dense.shape)
    cut = width // 128
    g_cross = jnp.transpose(tiles[:, :cut], (0, 2, 1, 3)).reshape(width, width)
    g_top = jnp.transpose(tiles[:, cut:], (0, 2, 1, 3)).reshape(width, top)
    vec = vecs.reshape(-1)
    return (logits[0], g_cross, g_top, vec[:width], vec[width:width + top], vec[width + top:], table_grad)


def solution(mesh):
    placed = (
        P("shard", None),
        P(),
        P(),
        P(),
        P(),
        P(),
        P(("dp", "shard"), None, None),
        P(("dp", "shard"), None, None),
        P(("dp", "shard"), None),
        P(("dp", "shard")),
    )
    return jax.shard_map(
        on_device,
        mesh=mesh,
        in_specs=placed,
        out_specs=(P(("dp", "shard")), P(), P(), P(), P(), P(), P("shard", None)),
        check_vma=False,
    )
```

time: 661 us -> 270 us (0.41)
  waiting for transfers between devices: 288 us -> 0 us
  Pallas kernels: 0 us -> 257 us
  other arithmetic: 135 us -> 0 us
  local copies, waits for them, and re-layouts: 102 us -> 11.6 us
  blocking collectives: 81 us -> 0 us
  starting transfers between devices: 24.8 us -> 0 us
  matrix products: 14.7 us -> 0 us
  between operations: 14.4 us -> 0.65 us
    pallas_call x0 -> x3, Pallas kernels: none -> 257 us  [the longest x1 130 us: reduce_all(): pl.pallas_call(body, out_shape=[jax.ShapeDtypeStruct((rows, emb), F32), j...]
    psum x2 -> x0, waiting for transfers between devices: 207 us -> none  [the longest x1 138 us: on_device(): lax.psum((g_cross, g_top, g_cbias, g_tbias, g_out), ('dp', 'shard'))]
    scatter-add x2 -> x0, other arithmetic: 121 us -> none  [the longest x1 97.5 us: on_device(): jnp.zeros(cache_flat.shape, jnp.float32).at[slots.reshape(-1)]]
    all_to_all x3 -> x0, waiting for transfers between devices: 81.1 us -> none  [the longest x1 43 us: on_device(): lax.all_to_all(slot_grads.reshape(cache.shape), 'shard', split_axis=0, co...]
    psum x1 -> x0, blocking collectives: 81 us -> none  [on_device(): lax.psum((g_cross, g_top, g_cbias, g_tbias, g_out), ('dp', 'shard'))]
    gather x2 -> x0, local copies, waits for them, and re-layouts: 70.3 us -> none  [the longest x1 56.1 us: on_device(): gathered = cache_flat[slots]]
    all_to_all x3 -> x0, starting transfers between devices: 24.7 us -> none  [the longest x1 12.3 us: on_device(): lax.all_to_all(requests, 'shard', split_axis=0, concat_axis=0, tiled=True)]
    dot_general x8 -> x0, matrix products: 14.7 us -> none  [the longest x1 3.98 us: on_device(): g_top = jnp.dot(hidden.T, dzb, preferred_element_type=jnp.float32)]
  transfers between devices with their start and end apart: 5 -> 0, of which waited for: 5 -> 0; matrix products, arithmetic and copies ran while one was open for 8% -> 0% of each run, Pallas kernels for 0% -> 0%
where the time goes in v2:
time: 270 us
  Pallas kernels  257 us (95%)
  local copies, waits for them, and re-layouts  11.6 us (4%)
    pallas_call x1, Pallas kernels, reduce_all(): pl.pallas_call(body, out_shape=[jax.ShapeDtypeStruct((rows, emb), F32), j...  130 us
    pallas_call x1, Pallas kernels, fetch(): pl.pallas_call(functools.partial(fetch_kernel, n, ny), out_shape=[jax.Sha...  69 us
    pallas_call x1, Pallas kernels, local_step(): pl.pallas_call(local_kernel, out_shape=out, in_specs=[vm] * 9, out_specs=...  58.2 us

profile of v2, /device:TPU:1, one launch (start us, length us, event | category | flops | bytes accessed | tf_op | source)
XLA Modules:
  0.0 269.5 jit_solution(18035739083614263090)
XLA Ops:
  0.6 69.0 %fetch_rows.1 = (f32[32,128,128]{2,1,0:T(8,128)}, s32[32,1,128]{2,1,0:T(1,128)}) custom-call(s32[32,1,128]{2,1,0:T(1,128)} %bitcast.28, f32[2048,128]{1,0:T(8,128)} %table.1), custom_call_target="tpu_custom_call" | custom-call | tf_op jit(solution)/shard_map/fetch_rows/pallas_call | solution.py:316
  69.6 58.2 %local_step.1 = (f32[1,512]{1,0:T(1,128)}, f32[128,12,8,128]{3,2,1,0:T(8,128)}, f32[16,128]{1,0:T(8,128)}, f32[32,128,128]{2,1,0:T(8,128)}) custom-call(f32[32,128,128]{2,1,0:T(8,128)} %get-tuple-element.16.cache, s32[8,4,512]{2,1,0:T(4,128)} %bitcast.27, s32[8,512]{1,0:T(8,128)} %bitcast.29, f32[1,512]{1,0:T(1,128)} %bitcast.31, bf16[1024,1024]{1,0:T(8,128)(2,1)} %cw.1, ...), custom_call_target="tpu_custom_call" | custom-call | tf_op jit(solution)/shard_map/local_step/pallas_call | solution.py:218
  127.8 130.2 %reduce_all.1 = (f32[2048,128]{1,0:T(8,128)}, f32[1536,8,128]{2,1,0:T(8,128)}, f32[16,128]{1,0:T(8,128)}) custom-call(f32[32,128,128]{2,1,0:T(8,128)} %get-tuple-element.18.refs_0_, s32[32,1,128]{2,1,0:T(1,128)} %get-tuple-element.19.refs_1_, f32[1536,8,128]{2,1,0:T(8,128)} %bitcast.24, f32[16,128]{1,0:T(8,128)} %get-tuple-element.21.refs_3_), custom_call_target="tpu_custom_call" | custom-call | tf_op jit(solution)/shard_map/reduce_all/pallas_call | solution.py:602
  257.9 1.3 slice_bitcast_fusion.2
  259.2 1.3 slice_bitcast_fusion.3
  260.6 3.1 %slice_bitcast_fusion.1 = f32[1024,512]{1,0:T(8,128)} fusion(f32[128,12,8,128]{3,2,1,0:T(8,128)} %bitcast.25), kind=kLoop, calls=%fused_computation.1 | loop fusion | bytes 4194304 | tf_op jit(solution)/shard_map/reshape | solution.py:651
  263.7 0.0 copy-start
  263.7 4.9 %slice_bitcast_fusion = f32[1024,1024]{1,0:T(8,128)} fusion(f32[128,12,8,128]{3,2,1,0:T(8,128)} %bitcast.26), kind=kLoop, calls=%fused_computation | loop fusion | bytes 8388608 | tf_op jit(solution)/shard_map/reshape | solution.py:650
  268.6 0.0 copy-done
  268.6 1.0 copy.18
Async XLA Ops:
  263.7 4.9 %copy-start = (f32[2048,128]{1,0:T(8,128)S(1)}, f32[2048,128]{1,0:T(8,128)}, u32[]{:S(2)}) copy-start(f32[2048,128]{1,0:T(8,128)} %get-tuple-element.40) | copy-start | bytes 3145732

commit v3 on v0

v3 whole, which is shorter than its diff:
```python
import functools

import jax
import jax.numpy as jnp
from jax import lax
from jax.experimental import pallas as pl
from jax.experimental.pallas import tpu as pltpu
from jax.sharding import PartitionSpec as P

F32, BF16, I32 = jnp.float32, jnp.bfloat16, jnp.int32
VMEM_LIMIT = 60 * 1024 * 1024
NX, NY = 4, 4
NN = ((1,), (0,))
NT = ((1,), (1,))
TN = ((0,), (0,))


def dot(a, b, dims):
    return lax.dot_general(a, b, (dims, ((), ())), preferred_element_type=F32)


def split(x):
    hi = x.astype(BF16)
    lo = (x - hi.astype(F32)).astype(BF16)
    return jnp.concatenate([hi, lo], axis=1)


def nibble_mask(o):
    return jnp.left_shift(jnp.int32(15), (o % 8) * 4)


def nibble_scale(o):
    k = o % 8
    s = jnp.where((k & 1) == 1, F32(2.0**-4), F32(1.0))
    s = s * jnp.where((k & 2) == 2, F32(2.0**-8), F32(1.0))
    return s * jnp.where((k & 4) == 4, F32(2.0**-16), F32(1.0))


def key_codes(slots, lengths, rowcode, rowbit):
    feats, bag, samples = slots.shape
    for b in range(bag):
        slot = slots[:, b, :]
        owner = slot >> 7
        rowcode[pl.ds(b * feats, feats), :] = jnp.where(
            lengths[...] > b, (slot & 127) + ((owner >> 3) << 7), -1)
        rowbit[pl.ds(b * feats, feats), :] = jnp.left_shift(jnp.ones_like(owner), (owner & 7) << 2)


def count_words(words, feats, bag, code_of, bit_of, place):
    groups, cap = words.shape[0], 128
    for f in range(feats):
        sums = [jnp.zeros(place.shape, I32)] * groups
        for b in range(bag):
            key = b * feats + f
            code = jnp.broadcast_to(code_of(key), place.shape) - place
            bit = jnp.broadcast_to(bit_of(key), place.shape)
            for w in range(groups):
                sums[w] = sums[w] + jnp.where(code == w * cap, bit, 0)
        for w in range(groups):
            words[w, f] = sums[w]


def counts(word, o):
    return (word & nibble_mask(o)).astype(F32).astype(BF16)


class Group:
    def __init__(self, size, me, address):
        self.size, self.me, self.address = size, me, address

    def others(self):
        return [(d, (self.me + d) % self.size) for d in range(1, self.size)]


def plane_step(j, nz):
    return nz // 2 + (j // 2 + j % 2) * (1 - 2 * (j % 2))


def peer_of(k, me, ny, nz):
    z = (me // ny + plane_step(k // ny, nz)) % nz
    y = (me % ny + (k + 1) % ny) % ny
    return z * ny + y


def plane_from(j, z, nz):
    return (z - plane_step(j, nz) + 2 * nz) % nz


def remote(src, dst, send, recv, to):
    return pltpu.make_async_remote_copy(
        src_ref=src, dst_ref=dst, send_sem=send, recv_sem=recv, device_id=to)


def spread(group, src, dst, send, recv):
    copies = []
    for d, j in group.others():
        cp = remote(src(j), dst(group.me), send.at[d], recv.at[group.me], group.address(j))
        cp.start()
        copies.append(cp)
    return copies


def arrived(group, src, dst, send, recv):
    for d, j in group.others():
        remote(src(j), dst(j), send.at[d], recv.at[j], group.address(j)).wait_recv()


def fetch_kernel(n, ny, wanted, table, slots, lengths, x0, ids_in,
                 ids_sm, sendbuf, cache, words, rowcode, rowbit, colcode, colbit, acc,
                 id_send, id_recv, row_send, row_recv, sm_sem):
    nz = n // ny
    cap, emb = cache.shape[1:]
    feats, bag, samples = slots.shape
    me = lax.axis_index("shard")
    z = me // ny
    barrier = pltpu.get_barrier_semaphore()

    @pl.loop(0, n - 1)
    def _(k):
        pl.semaphore_signal(barrier, inc=1, device_id={"shard": peer_of(k, me, ny, nz)})

    pl.semaphore_wait(barrier, n - 1)

    def id_copy(p, slot):
        return remote(wanted.at[p], ids_in.at[slot], id_send.at[p], id_recv.at[slot], {"shard": p})

    def row_copy(p, slot):
        return remote(sendbuf.at[p], cache.at[slot], row_send.at[p], row_recv.at[slot], {"shard": p})

    @pl.loop(0, n - 1)
    def _(k):
        id_copy(peer_of(k, me, ny, nz), me).start()

    ids_in[me] = wanted[me]
    key_codes(slots, lengths, rowcode, rowbit)
    colcode[...] = rowcode[...].T
    colbit[...] = rowbit[...].T

    @pl.loop(0, n - 1)
    def _(k):
        p = peer_of(k, me, ny, nz)
        id_copy(p, p).wait_recv()

    to_smem = pltpu.make_async_copy(ids_in, ids_sm, sm_sem)
    to_smem.start()
    to_smem.wait()

    def serve(p, out):
        @pl.loop(0, cap // 16)
        def _(t):
            for i in range(16):
                row = t * 16 + i
                out[p, pl.ds(row, 1), :] = table[pl.ds(ids_sm[p, 0, row], 1), :]

    @pl.loop(0, n - 1)
    def _(k):
        p = peer_of(k, me, ny, nz)
        serve(p, sendbuf)
        row_copy(p, me).start()

    serve(me, cache)

    count_words(
        words, feats, bag, lambda key: colcode[:, key:key + 1], lambda key: colbit[:, key:key + 1],
        lax.broadcasted_iota(I32, (samples, cap), 1))

    @pl.loop(0, feats)
    def _(f):
        acc[f] = jnp.zeros(acc.shape[1:], F32)

    @pl.loop(0, nz)
    def _(j):
        first = plane_from(j, z, nz) * ny

        @pl.loop(0, ny)
        def _(i):
            p = first + i

            @pl.when(p != me)
            def _():
                row_copy(p, p).wait_recv()

        rhs = jnp.concatenate(
            [split(cache[first + i] * nibble_scale(first + i)) for i in range(ny)], axis=0)

        @pl.loop(0, feats)
        def _(f):
            word = words[first // 8, f]
            lhs = jnp.concatenate([counts(word, first + i) for i in range(ny)], axis=1)
            acc[f] = acc[f] + dot(lhs, rhs, NN)

    for f in range(feats):
        x0[:, f * emb:(f + 1) * emb] = (acc[f, :, :emb] + acc[f, :, emb:]).astype(BF16)

    @pl.loop(0, n - 1)
    def _(k):
        p = peer_of(k, me, ny, nz)
        id_copy(p, me).wait_send()
        row_copy(p, me).wait_send()


def fetch(wanted, table, slots, lengths, ny):
    n, cap = wanted.shape
    emb = table.shape[1]
    feats, bag, samples = slots.shape
    keys = feats * bag
    vm = pl.BlockSpec(memory_space=pltpu.VMEM)
    dma = pltpu.SemaphoreType.DMA
    return pl.pallas_call(
        functools.partial(fetch_kernel, n, ny),
        out_shape=[
            jax.ShapeDtypeStruct((samples, feats * emb), BF16),
            jax.ShapeDtypeStruct((n, 1, cap), I32),
        ],
        in_specs=[vm] * 4,
        out_specs=[vm] * 2,
        scratch_shapes=[
            pltpu.SMEM((n, 1, cap), I32),
            pltpu.VMEM((n, cap, emb), F32),
            pltpu.VMEM((n, cap, emb), F32),
            pltpu.VMEM((pl.cdiv(n, 8), feats, samples, cap), I32),
            pltpu.VMEM((keys, samples), I32),
            pltpu.VMEM((keys, samples), I32),
            pltpu.VMEM((samples, keys), I32),
            pltpu.VMEM((samples, keys), I32),
            pltpu.VMEM((feats, samples, 2 * emb), F32),
            dma((n,)), dma((n,)), dma((n,)), dma((n,)), dma,
        ],
        compiler_params=pltpu.CompilerParams(
            collective_id=0, has_side_effects=True, vmem_limit_bytes=VMEM_LIMIT),
        name="fetch_pool",
    )(wanted.reshape(n, 1, cap), table, slots, lengths)


def add_refs(out, parts, chunk):
    count = out.shape[0]
    chunk = min(chunk, count)

    @pl.loop(0, count // chunk)
    def _(t):
        w = pl.ds(t * chunk, chunk)
        total = parts[0][w]
        for p in parts[1:]:
            total = total + p[w]
        out[w] = total


class Stream:
    def __init__(self, local, out, h, core, first, second, gz, bufs, sems):
        self.local, self.out, self.h = local, out, h
        self.core, self.first, self.second, self.gz = core, first, second, gz
        self.r1, self.r2, self.b, self.r3, self.c, self.r4 = bufs
        self.sems = sems
        self.quarter = local.shape[0] // 4
        self.piece = self.quarter // first.size
        self.unit = self.piece // second.size
        self.pending = []

    def pair(self, k):
        return self.sems[0].at[k], self.sems[1].at[k]

    def go(self, group, src, dst, k):
        self.pending += spread(group, src, dst, *self.pair(k))

    def come(self, group, src, dst, k):
        arrived(group, src, dst, *self.pair(k))

    def half(self, ref, c):
        return ref.at[pl.ds((2 * c + self.h) * self.quarter, self.quarter)]

    def core_args(self):
        return self.core, lambda j: self.half(self.local, j), lambda i: self.r1, 0

    def first_args(self):
        return self.first, lambda j: self.r1.at[pl.ds(j * self.piece, self.piece)], lambda i: self.r2.at[i], 1

    def second_args(self):
        return self.second, lambda j: self.b.at[pl.ds(j * self.unit, self.unit)], lambda i: self.r3.at[i], 2

    def z_args(self):
        return self.gz, lambda j: self.c.at[:, j], lambda i: self.r4.at[i], 3

    def at(self, a=None, bb=None):
        at = (2 * self.core.me + self.h) * self.quarter
        if a is not None:
            at = at + a * self.piece
        if bb is not None:
            at = at + bb * self.unit
        return at

    def zback_args(self):
        here = lambda i: self.out.at[pl.ds(self.at(self.first.me, self.second.me), self.unit), i]
        return self.gz, lambda j: here(self.gz.me), here, 4

    def second_back_args(self):
        here = lambda i: self.out.at[pl.ds(self.at(self.first.me, i), self.unit)]
        return self.second, lambda j: here(self.second.me), here, 5

    def first_back_args(self):
        here = lambda i: self.out.at[pl.ds(self.at(i), self.piece)]
        return self.first, lambda j: here(self.first.me), here, 6

    def core_back_args(self):
        here = lambda i: self.half(self.out, i)
        return self.core, lambda j: here(self.core.me), here, 7

    def step(self, k):
        args = (self.core_args, self.first_args, self.second_args, self.z_args,
                self.zback_args, self.second_back_args, self.first_back_args, self.core_back_args)
        if k >= 0:
            group, src, dst, i = args[k]()
            self.come(group, src, dst, i)
            if k == 0:
                add_refs(self.r1, [self.r1, self.half(self.local, group.me)], 4)
            elif k < 4:
                out = (None, self.b, self.c, None)[k]
                if k == 3:
                    out = self.out.at[pl.ds(self.at(self.first.me, self.second.me), self.unit), self.gz.me]
                add_refs(out, [src(group.me)] + [dst(j) for _, j in group.others()], 2)
        if k + 1 < len(args):
            self.go(*args[k + 1]())


def dense_kernel(nx, ny, nz, x0, slots, lengths, cot, cw, cb, tw, tb, ow, served,
                 logits, table_out, cross_out, top_out, small_out,
                 g_cross, g_top, small, slot_grads, back, tsum, rt1, rt2,
                 words, rowcode, rowbit, y, h, dzb, dyb, dh, dxhl, bufs, sm_bufs, sems):
    n = ny * nz
    cap, emb = back.shape[1:]
    rows = tsum.shape[0]
    feats, bag, samples = slots.shape
    width, top = tw.shape
    dp, me = lax.axis_index("dp"), lax.axis_index("shard")
    x, core, z, yy = dp // 2, dp % 2, me // ny, me % ny
    gx = Group(nx, x, lambda j: {"dp": j * 2 + core})
    gy = Group(ny, yy, lambda j: {"shard": z * ny + j})
    gz = Group(nz, z, lambda j: {"shard": j * ny + yy})
    gc = Group(2, core, lambda j: {"dp": x * 2 + j})
    g_send, g_recv, t_send, t_recv, sm_send, sm_recv, d_send, d_recv = sems

    barrier = pltpu.get_barrier_semaphore()

    @pl.loop(0, n - 1)
    def _(k):
        pl.semaphore_signal(barrier, inc=1, device_id={"shard": peer_of(k, me, ny, nz)})

    for grp in (gx, gc):
        for _, j in grp.others():
            pl.semaphore_signal(barrier, inc=1, device_id=grp.address(j))

    streams = []
    for a, (local, out) in enumerate(((g_top, top_out), (g_cross, cross_out))):
        for hh in range(2):
            first, second = ((gx, gy), (gy, gx))[hh]
            s = 2 * a + hh
            streams.append(Stream(local, out, hh, gc, first, second, gz, bufs[6 * s:6 * s + 6],
                                  (d_send.at[s], d_recv.at[s])))
    tops, crosses = streams[:2], streams[2:]

    step = min(256, width)
    lanes = step // 128

    def put_small(at, vec):
        for t in range(lanes):
            small[pl.ds(at + t, 1), :] = vec[:, t * 128:(t + 1) * 128]

    def put_dense(out, j, val):
        per = val.shape[1] // 128
        deep = nz // per
        count = step // 8 // deep
        for t in range(per):
            v = val[:, t * 128:(t + 1) * 128].reshape(count, deep, 8, 128)
            for i in range(deep):
                out[pl.ds(j * count, count), i * per + t] = v[:, i]

    @pl.loop(0, width // step)
    def _(j):
        c = pl.ds(pl.multiple_of(j * step, step), step)
        yv = dot(x0[...], cw[:, c], NN) + cb[:, c]
        y[:, c] = yv
        xf = x0[:, c].astype(F32)
        h[:, c] = (xf * yv + xf).astype(BF16)

    cotb = jnp.broadcast_to(cot[...], (128, samples)).T
    lsum = jnp.zeros((samples, 128), F32)
    tstep = min(256, top)
    for j in range(top // tstep):
        c = pl.ds(j * tstep, tstep)
        zv = dot(h[...], tw[:, c], NN) + tb[:, c]
        sig = jax.nn.sigmoid(zv)
        u = zv * sig
        uw = u * ow[:, c]
        cotw = jnp.concatenate([cotb] * (tstep // 128), axis=1)
        for t in range(tstep // 128):
            lsum = lsum + uw[:, t * 128:(t + 1) * 128]
        gow = jnp.sum(u * cotw, axis=0, keepdims=True)
        dz = cotw * ow[:, c] * (sig * (1.0 + zv * (1.0 - sig)))
        gtb = jnp.sum(dz, axis=0, keepdims=True)
        for t in range(tstep // 128):
            at = width // 128 + j * (tstep // 128) + t
            small[pl.ds(at, 1), :] = gtb[:, t * 128:(t + 1) * 128]
            small[pl.ds(at + top // 128, 1), :] = gow[:, t * 128:(t + 1) * 128]
        dzb[:, c] = dz.astype(BF16)
    logits[...] = jnp.sum(lsum.T, axis=0, keepdims=True)

    @pl.loop(0, width // step)
    def _(j):
        c = pl.ds(pl.multiple_of(j * step, step), step)
        put_dense(g_top, j, dot(h[:, c], dzb[...], TN))

    pl.semaphore_wait(barrier, n - 1 + nx - 1 + 1)
    for s in tops:
        s.step(-1)

    @pl.loop(0, width // step)
    def _(j):
        c = pl.ds(pl.multiple_of(j * step, step), step)
        dhv = dot(dzb[...], tw[c, :], NT)
        dh[:, c] = dhv
        dy = dhv * x0[:, c].astype(F32)
        put_small(j * lanes, jnp.sum(dy, axis=0, keepdims=True))
        dyb[:, c] = dy.astype(BF16)

    @pl.loop(0, width // step)
    def _(j):
        c = pl.ds(pl.multiple_of(j * step, step), step)
        put_dense(g_cross, j, dot(x0[:, c], dyb[...], TN))

    for s in crosses:
        s.step(-1)
    pending = []
    s_core, s_x, s_y, s_z, sm1, sm2, sm3 = sm_bufs

    def small_go(k, grp, src, slots_):
        slots_[grp.me] = src[...]
        args = (grp, lambda j: src, lambda i: slots_.at[i], sm_send.at[k], sm_recv.at[k])
        pending.extend(spread(*args))
        return args

    def small_come(args, slots_, out):
        arrived(*args)
        total = slots_[0]
        for i in range(1, slots_.shape[0]):
            total = total + slots_[i]
        out[...] = total

    sm_args = small_go(0, gc, small, s_core)

    @pl.loop(0, width // step)
    def _(j):
        c = pl.ds(pl.multiple_of(j * step, step), step)
        dx = dh[:, c] * (y[:, c] + 1.0) + dot(dyb[...], cw[c, :], NT)
        for t in range(step // emb):
            dxhl[j * (step // emb) + t] = split(dx[:, t * emb:(t + 1) * emb])

    for s in tops:
        s.step(0)
    key_codes(slots, lengths, rowcode, rowbit)
    count_words(
        words, feats, bag, lambda key: rowcode[key:key + 1, :], lambda key: rowbit[key:key + 1, :],
        lax.broadcasted_iota(I32, (cap, samples), 0))
    for s in crosses:
        s.step(0)
    small_come(sm_args, s_core, sm1)
    sm_args = small_go(1, gx, sm1, s_x)

    def grad_copy(p, slot):
        return remote(slot_grads.at[p], back.at[slot], g_send.at[p], g_recv.at[slot], {"shard": p})

    def slot_plane(j):
        first = ((z + plane_step(j, nz)) % nz) * ny
        total = jnp.zeros((ny * cap, 2 * emb), F32)
        for f in range(feats):
            word = words[first // 8, f]
            lhs = jnp.concatenate([counts(word, first + i) for i in range(ny)], axis=0)
            total = total + dot(lhs, dxhl[f], NN)
        for i in range(ny):
            part = total[i * cap:(i + 1) * cap]
            slot_grads[first + i] = (part[:, :emb] + part[:, emb:]) * nibble_scale(first + i)

        @pl.loop(0, ny)
        def _(i):
            p = first + (yy + i + 1) % ny

            @pl.when(p != me)
            def _():
                grad_copy(p, me).start()

    @pl.loop(0, nz // 2)
    def _(j):
        slot_plane(j)

    for s in tops:
        s.step(1)

    @pl.loop(nz // 2, nz)
    def _(j):
        slot_plane(j)

    back[me] = slot_grads[me]

    for s in crosses:
        s.step(1)
    small_come(sm_args, s_x, sm2)
    sm_args = small_go(2, gy, sm2, s_y)
    for s in tops:
        s.step(2)
    for s in crosses:
        s.step(2)
    small_come(sm_args, s_y, sm3)
    sm_args = small_go(3, gz, sm3, s_z)
    for s in tops:
        s.step(3)
    for s in crosses:
        s.step(3)
    for s in tops:
        s.step(4)
    for s in crosses:
        s.step(4)
    small_come(sm_args, s_z, small_out)

    def owner_plane(j):
        first = plane_from(j, z, nz) * ny

        @pl.loop(0, ny)
        def _(i):
            p = first + i

            @pl.when(p != me)
            def _():
                grad_copy(p, p).wait_recv()

        rhs = jnp.concatenate([split(back[first + i]) for i in range(ny)], axis=0)
        ids = jnp.concatenate([served[first + i] for i in range(ny)], axis=1)
        mstep = min(512, rows)

        @pl.loop(0, rows // mstep)
        def _(t):
            at = t * mstep
            row = lax.broadcasted_iota(I32, (mstep, ny * cap), 0) + at
            hot = jnp.where(row == ids, F32(1), F32(0)).astype(BF16)
            part = dot(hot, rhs, NN)
            part = part[:, :emb] + part[:, emb:]
            w = pl.ds(pl.multiple_of(at, mstep), mstep)
            tsum[w] = jnp.where(j == 0, part, tsum[w] + part)

    @pl.loop(0, nz // 2)
    def _(j):
        owner_plane(j)

    for s in tops:
        s.step(5)
    for s in crosses:
        s.step(5)

    @pl.loop(nz // 2, nz)
    def _(j):
        owner_plane(j)

    thalf = rows // 2
    tq = thalf // nx
    rows_at = lambda ref, at, size: ref.at[pl.ds(pl.multiple_of(at, size), size)]
    tside = lambda ref, i: rows_at(ref, i * thalf, thalf)
    tpart = lambda ref, i: rows_at(ref, i * tq, tq)
    sem = lambda k: (t_send.at[k], t_recv.at[k])
    tc = (gc, lambda j: tside(tsum, j), lambda i: rt1, *sem(0))
    pending += spread(*tc)
    for s in tops:
        s.step(6)
    arrived(*tc)
    rt1[...] = rt1[...] + tside(tsum, core)[...]
    tx = (gx, lambda j: tpart(rt1, j), lambda i: rt2.at[i], *sem(1))
    pending += spread(*tx)
    for s in crosses:
        s.step(6)
    arrived(*tx)
    mine = tpart(tside(table_out, core), x)
    total = tpart(rt1, x)[...]
    for _, j in gx.others():
        total = total + rt2[j]
    mine[...] = total
    there = lambda i: rows_at(table_out, core * thalf + i * tq, tq)
    tb_ = (gx, lambda j: there(x), there, *sem(2))
    pending += spread(*tb_)
    arrived(*tb_)
    tcb = (gc, lambda j: tside(table_out, core), lambda i: tside(table_out, i), *sem(3))
    pending += spread(*tcb)
    for s in streams:
        s.step(7)
    arrived(*tcb)

    for cp in pending + [cp for s in streams for cp in s.pending]:
        cp.wait_send()

    @pl.loop(0, n - 1)
    def _(k):
        grad_copy(peer_of(k, me, ny, nz), me).wait_send()


def dense_and_reduce(x0, slots, lengths, cot, cw, cb, tw, tb, ow, served, nx, ny, rows):
    samples, width = x0.shape
    top = tw.shape[1]
    feats, bag, _ = slots.shape
    n, _, cap = served.shape
    emb = width // feats
    nz = n // ny
    keys = feats * bag
    vm = pl.BlockSpec(memory_space=pltpu.VMEM)
    v = pltpu.VMEM
    dma = lambda *s: pltpu.SemaphoreType.DMA(s)
    tiles = lambda *lead: (*lead, 8, 128)
    r_cross = width // 8 * (width // 128) // nz
    r_top = width // 8 * (top // 128) // nz
    sm = ((width + 2 * top) // 128, 128)
    most = max(nx, ny, nz)

    bufs = []
    for r in (r_top, r_cross):
        for a, b in ((nx, ny), (ny, nx)):
            q = r // 4
            p = q // a
            u = p // b
            bufs += [v(tiles(q, nz), F32), v(tiles(a, p, nz), F32), v(tiles(p, nz), F32),
                     v(tiles(b, u, nz), F32), v(tiles(u, nz), F32), v(tiles(nz, u), F32)]
    sm_bufs = [v((k, *sm), F32) for k in (2, nx, ny, nz)] + [v(sm, F32)] * 3
    sems = [dma(n), dma(n), dma(4, most), dma(4, most), dma(4, most), dma(4, most), dma(4, 8, most), dma(4, 8, most)]
    own = [
        v(tiles(r_cross, nz), F32), v(tiles(r_top, nz), F32), v(sm, F32),
        v((n, cap, emb), F32), v((n, cap, emb), F32), v((rows, emb), F32),
        v((rows // 2, emb), F32), v((nx, rows // 2 // nx, emb), F32),
        v((pl.cdiv(n, 8), feats, cap, samples), I32), v((keys, samples), I32), v((keys, samples), I32),
        v((samples, width), F32), v((samples, width), BF16), v((samples, top), BF16), v((samples, width), BF16),
        v((samples, width), F32), v((feats, samples, 2 * emb), BF16),
    ]

    def body(*refs):
        head, rest = refs[:15 + len(own)], refs[15 + len(own):]
        dense_kernel(nx, ny, nz, *head, rest[:24], rest[24:31], rest[31:])

    return pl.pallas_call(
        body,
        out_shape=[
            jax.ShapeDtypeStruct((1, samples), F32),
            jax.ShapeDtypeStruct((rows, emb), F32),
            jax.ShapeDtypeStruct(tiles(r_cross, nz), F32),
            jax.ShapeDtypeStruct(tiles(r_top, nz), F32),
            jax.ShapeDtypeStruct(sm, F32),
        ],
        in_specs=[vm] * 10,
        out_specs=[vm] * 5,
        scratch_shapes=own + bufs + sm_bufs + sems,
        compiler_params=pltpu.CompilerParams(
            collective_id=1, has_side_effects=True, vmem_limit_bytes=VMEM_LIMIT),
        name="dense_reduce",
    )(x0, slots, lengths, cot, cw, cb, tw, tb, ow, served)


def from_tiles(tiles, rows, columns):
    return jnp.transpose(tiles.reshape(rows // 8, columns // 128, 8, 128), (0, 2, 1, 3)).reshape(rows, columns)


def on_device(table, cross_weight, cross_bias, top_weight, top_bias, out_weight, wanted, slots, lengths, logit_grad,
              nx=NX, ny=NY):
    width, top = top_weight.shape
    keys, live = jnp.transpose(slots, (1, 2, 0)), lengths.T
    x0, served = fetch(wanted[0], table, keys, live, ny)
    logits, table_grad, cross, tops, vecs = dense_and_reduce(
        x0, keys, live, logit_grad[None], cross_weight, cross_bias[None], top_weight, top_bias[None], out_weight[None],
        served, nx, ny, table.shape[0])
    vec = vecs.reshape(-1)
    return (logits[0], from_tiles(cross, width, width), from_tiles(tops, width, top),
            vec[:width], vec[width:width + top], vec[width + top:], table_grad)


def solution(mesh):
    placed = (
        P("shard", None),
        P(),
        P(),
        P(),
        P(),
        P(),
        P(("dp", "shard"), None, None),
        P(("dp", "shard"), None, None),
        P(("dp", "shard"), None),
        P(("dp", "shard")),
    )
    return jax.shard_map(
        on_device,
        mesh=mesh,
        in_specs=placed,
        out_specs=(P(("dp", "shard")), P(), P(), P(), P(), P(), P("shard", None)),
        check_vma=False,
    )
```

time: 661 us -> 222 us (0.34)
  waiting for transfers between devices: 288 us -> 0 us
  Pallas kernels: 0 us -> 209 us
  other arithmetic: 135 us -> 0 us
  local copies, waits for them, and re-layouts: 102 us -> 11.7 us
  blocking collectives: 81 us -> 0 us
  starting transfers between devices: 24.8 us -> 0 us
  matrix products: 14.7 us -> 0 us
  between operations: 14.4 us -> 0.65 us
    pallas_call x0 -> x2, Pallas kernels: none -> 209 us  [the longest x1 133 us: dense_and_reduce(): pl.pallas_call(body, out_shape=[jax.ShapeDtypeStruct((1, samples), F32),...]
    psum x2 -> x0, waiting for transfers between devices: 207 us -> none  [the longest x1 138 us: on_device(): lax.psum((g_cross, g_top, g_cbias, g_tbias, g_out), ('dp', 'shard'))]
    scatter-add x2 -> x0, other arithmetic: 121 us -> none  [the longest x1 97.5 us: on_device(): jnp.zeros(cache_flat.shape, jnp.float32).at[slots.reshape(-1)]]
    all_to_all x3 -> x0, waiting for transfers between devices: 81.1 us -> none  [the longest x1 43 us: on_device(): lax.all_to_all(slot_grads.reshape(cache.shape), 'shard', split_axis=0, co...]
    psum x1 -> x0, blocking collectives: 81 us -> none  [on_device(): lax.psum((g_cross, g_top, g_cbias, g_tbias, g_out), ('dp', 'shard'))]
    gather x2 -> x0, local copies, waits for them, and re-layouts: 70.3 us -> none  [the longest x1 56.1 us: on_device(): gathered = cache_flat[slots]]
    all_to_all x3 -> x0, starting transfers between devices: 24.7 us -> none  [the longest x1 12.3 us: on_device(): lax.all_to_all(requests, 'shard', split_axis=0, concat_axis=0, tiled=True)]
    dot_general x8 -> x0, matrix products: 14.7 us -> none  [the longest x1 3.98 us: on_device(): g_top = jnp.dot(hidden.T, dzb, preferred_element_type=jnp.float32)]
  transfers between devices with their start and end apart: 5 -> 0, of which waited for: 5 -> 0; matrix products, arithmetic and copies ran while one was open for 8% -> 0% of each run, Pallas kernels for 0% -> 0%
where the time goes in v3:
time: 222 us
  Pallas kernels  209 us (94%)
  local copies, waits for them, and re-layouts  11.7 us (5%)
    pallas_call x1, Pallas kernels, dense_and_reduce(): pl.pallas_call(body, out_shape=[jax.ShapeDtypeStruct((1, samples), F32),...  133 us
    pallas_call x1, Pallas kernels, fetch(): pl.pallas_call(functools.partial(fetch_kernel, n, ny), out_shape=[jax.Sha...  76.7 us
    unnamed x8, local copies, waits for them, and re-layouts  9.12 us

profile of v3, /device:TPU:1, one launch (start us, length us, event | category | flops | bytes accessed | tf_op | source)
XLA Modules:
  0.0 221.6 jit_solution(7714212226267696714)
XLA Ops:
  0.6 76.7 %fetch_pool.1 = (bf16[512,1024]{1,0:T(8,128)(2,1)}, s32[32,1,128]{2,1,0:T(1,128)}) custom-call(s32[32,1,128]{2,1,0:T(1,128)} %bitcast.28, f32[2048,128]{1,0:T(8,128)} %table.1, s32[8,4,512]{2,1,0:T(4,128)} %bitcast.24, s32[8,512]{1,0:T(8,128)} %bitcast.26), custom_call_target="tpu_custom_call" | custom-call | tf_op jit(solution)/shard_map/fetch_pool/pallas_call | solution.py:209
  77.3 132.6 %dense_reduce.1 = (f32[1,512]{1,0:T(1,128)}, f32[2048,128]{1,0:T(8,128)}, f32[128,8,8,128]{3,2,1,0:T(8,128)}, f32[64,8,8,128]{3,2,1,0:T(8,128)}, f32[16,128]{1,0:T(8,128)}) custom-call(bf16[512,1024]{1,0:T(8,128)(2,1)} %get-tuple-element.14.refs_0_, s32[8,4,512]{2,1,0:T(4,128)} %bitcast.25, s32[8,512]{1,0:T(8,128)} %bitcast.27, f32[1,512]{1,0:T(1,128)} %bitcast.30, ...), custom_call_target="tpu_custom_call" | custom-call | tf_op jit(solution)/shard_map/dense_reduce/pallas_call | solution.py:640
  209.9 1.3 slice_bitcast_fusion
  211.2 1.3 slice_bitcast_fusion.1
  212.5 1.3 copy.21
  213.8 0.0 copy-start
  213.8 4.9 %copy.22 = f32[1024,1024]{1,0:T(8,128)} copy(f32[1024,1024]{1,0:T(8,128)} %bitcast.22) | data formatting | bytes 8388608
  218.7 0.0 copy-done
  218.7 0.0 copy-start.1
  218.7 1.3 copy.23
  220.0 0.6 copy-done.1
  220.7 1.0 copy.24
Async XLA Ops:
  213.8 4.9 %copy-start = (f32[64,8,8,128]{3,2,1,0:T(8,128)S(1)}, f32[64,8,8,128]{3,2,1,0:T(8,128)}, u32[]{:S(2)}) copy-start(f32[64,8,8,128]{3,2,1,0:T(8,128)} %get-tuple-element.18) | copy-start | bytes 6291460
  218.7 2.0 copy-start.1

commit v4 on v3

--- a/solution.py
+++ b/solution.py
@@ -1,4 +1,5 @@
 import functools
+import math
 
 import jax
 import jax.numpy as jnp
@@ -73,17 +74,21 @@
 
 
 def plane_step(j, nz):
+    return ((j + 1) // 2 * (2 * (j % 2) - 1) + nz) % nz
+
+
+def far_step(j, nz):
     return nz // 2 + (j // 2 + j % 2) * (1 - 2 * (j % 2))
 
 
 def peer_of(k, me, ny, nz):
-    z = (me // ny + plane_step(k // ny, nz)) % nz
+    z = (me // ny + plane_step((k + 1) // ny, nz)) % nz
     y = (me % ny + (k + 1) % ny) % ny
     return z * ny + y
 
 
-def plane_from(j, z, nz):
-    return (z - plane_step(j, nz) + 2 * nz) % nz
+def plane_from(step, z, nz):
+    return (z - step + 2 * nz) % nz
 
 
 def remote(src, dst, send, recv, to):
@@ -105,9 +110,9 @@
         remote(src(j), dst(j), send.at[d], recv.at[j], group.address(j)).wait_recv()
 
 
-def fetch_kernel(n, ny, wanted, table, slots, lengths, x0, ids_in,
-                 ids_sm, sendbuf, cache, words, rowcode, rowbit, colcode, colbit, acc,
-                 id_send, id_recv, row_send, row_recv, sm_sem):
+def fetch_kernel(n, ny, wanted, table, slots, lengths, x0, ids_in, words_out,
+                 ids_sm, sendbuf, cache, words, wordst, rowcode, rowbit, colcode, colbit, acc,
+                 id_send, id_recv, row_send, row_recv, sm_sem, words_sem):
     nz = n // ny
     cap, emb = cache.shape[1:]
     feats, bag, samples = slots.shape
@@ -168,9 +173,15 @@
     def _(f):
         acc[f] = jnp.zeros(acc.shape[1:], F32)
 
+    count_words(
+        wordst, feats, bag, lambda key: rowcode[key:key + 1, :], lambda key: rowbit[key:key + 1, :],
+        lax.broadcasted_iota(I32, (cap, samples), 0))
+    words_copy = pltpu.make_async_copy(wordst, words_out, words_sem)
+    words_copy.start()
+
     @pl.loop(0, nz)
     def _(j):
-        first = plane_from(j, z, nz) * ny
+        first = plane_from(plane_step(j, nz), z, nz) * ny
 
         @pl.loop(0, ny)
         def _(i):
@@ -197,6 +208,8 @@
         p = peer_of(k, me, ny, nz)
         id_copy(p, me).wait_send()
         row_copy(p, me).wait_send()
+
+    words_copy.wait()
 
 
 def fetch(wanted, table, slots, lengths, ny):
@@ -211,20 +224,22 @@
         out_shape=[
             jax.ShapeDtypeStruct((samples, feats * emb), BF16),
             jax.ShapeDtypeStruct((n, 1, cap), I32),
+            jax.ShapeDtypeStruct((pl.cdiv(n, 8), feats, cap, samples), I32),
         ],
         in_specs=[vm] * 4,
-        out_specs=[vm] * 2,
+        out_specs=[vm, vm, pl.BlockSpec(memory_space=pl.ANY)],
         scratch_shapes=[
             pltpu.SMEM((n, 1, cap), I32),
             pltpu.VMEM((n, cap, emb), F32),
             pltpu.VMEM((n, cap, emb), F32),
             pltpu.VMEM((pl.cdiv(n, 8), feats, samples, cap), I32),
+            pltpu.VMEM((pl.cdiv(n, 8), feats, cap, samples), I32),
             pltpu.VMEM((keys, samples), I32),
             pltpu.VMEM((keys, samples), I32),
             pltpu.VMEM((samples, keys), I32),
             pltpu.VMEM((samples, keys), I32),
             pltpu.VMEM((feats, samples, 2 * emb), F32),
-            dma((n,)), dma((n,)), dma((n,)), dma((n,)), dma,
+            dma((n,)), dma((n,)), dma((n,)), dma((n,)), dma, dma,
         ],
         compiler_params=pltpu.CompilerParams(
             collective_id=0, has_side_effects=True, vmem_limit_bytes=VMEM_LIMIT),
@@ -234,7 +249,7 @@
 
 def add_refs(out, parts, chunk):
     count = out.shape[0]
-    chunk = min(chunk, count)
+    chunk = math.gcd(chunk, count)
 
     @pl.loop(0, count // chunk)
     def _(t):
@@ -245,14 +260,21 @@
         out[w] = total
 
 
+def shares(r, nx, ny):
+    per = r // 2
+    unit = nx * ny
+    second = max(unit, per // 4 // unit * unit)
+    return per - second, second
+
+
 class Stream:
-    def __init__(self, local, out, h, core, first, second, gz, bufs, sems):
-        self.local, self.out, self.h = local, out, h
+    def __init__(self, local, out, start, size, core, first, second, gz, bufs, sems):
+        self.local, self.out, self.start, self.size = local, out, start, size
         self.core, self.first, self.second, self.gz = core, first, second, gz
         self.r1, self.r2, self.b, self.r3, self.c, self.r4 = bufs
         self.sems = sems
-        self.quarter = local.shape[0] // 4
-        self.piece = self.quarter // first.size
+        self.share = local.shape[0] // 2
+        self.piece = size // first.size
         self.unit = self.piece // second.size
         self.pending = []
 
@@ -266,7 +288,7 @@
         arrived(group, src, dst, *self.pair(k))
 
     def half(self, ref, c):
-        return ref.at[pl.ds((2 * c + self.h) * self.quarter, self.quarter)]
+        return ref.at[pl.ds(c * self.share + self.start, self.size)]
 
     def core_args(self):
         return self.core, lambda j: self.half(self.local, j), lambda i: self.r1, 0
@@ -281,7 +303,7 @@
         return self.gz, lambda j: self.c.at[:, j], lambda i: self.r4.at[i], 3
 
     def at(self, a=None, bb=None):
-        at = (2 * self.core.me + self.h) * self.quarter
+        at = self.core.me * self.share + self.start
         if a is not None:
             at = at + a * self.piece
         if bb is not None:
@@ -321,14 +343,14 @@
             self.go(*args[k + 1]())
 
 
-def dense_kernel(nx, ny, nz, x0, slots, lengths, cot, cw, cb, tw, tb, ow, served,
+def dense_kernel(nx, ny, nz, x0, words_in, cot, cw, cb, tw, tb, ow, served,
                  logits, table_out, cross_out, top_out, small_out,
                  g_cross, g_top, small, slot_grads, back, tsum, rt1, rt2,
-                 words, rowcode, rowbit, y, h, dzb, dyb, dh, dxhl, bufs, sm_bufs, sems):
+                 words, y, h, dzb, dyb, dh, dxhl, bufs, sm_bufs, sems):
     n = ny * nz
     cap, emb = back.shape[1:]
     rows = tsum.shape[0]
-    feats, bag, samples = slots.shape
+    feats, samples = dxhl.shape[:2]
     width, top = tw.shape
     dp, me = lax.axis_index("dp"), lax.axis_index("shard")
     x, core, z, yy = dp // 2, dp % 2, me // ny, me % ny
@@ -336,7 +358,9 @@
     gy = Group(ny, yy, lambda j: {"shard": z * ny + j})
     gz = Group(nz, z, lambda j: {"shard": j * ny + yy})
     gc = Group(2, core, lambda j: {"dp": x * 2 + j})
-    g_send, g_recv, t_send, t_recv, sm_send, sm_recv, d_send, d_recv = sems
+    g_send, g_recv, t_send, t_recv, sm_send, sm_recv, d_send, d_recv, words_sem = sems
+    words_copy = pltpu.make_async_copy(words_in, words, words_sem)
+    words_copy.start()
 
     barrier = pltpu.get_barrier_semaphore()
 
@@ -353,7 +377,8 @@
         for hh in range(2):
             first, second = ((gx, gy), (gy, gx))[hh]
             s = 2 * a + hh
-            streams.append(Stream(local, out, hh, gc, first, second, gz, bufs[6 * s:6 * s + 6],
+            part = shares(local.shape[0], nx, ny)
+            streams.append(Stream(local, out, hh * part[0], part[hh], gc, first, second, gz, bufs[6 * s:6 * s + 6],
                                   (d_send.at[s], d_recv.at[s])))
     tops, crosses = streams[:2], streams[2:]
 
@@ -455,10 +480,7 @@
 
     for s in tops:
         s.step(0)
-    key_codes(slots, lengths, rowcode, rowbit)
-    count_words(
-        words, feats, bag, lambda key: rowcode[key:key + 1, :], lambda key: rowbit[key:key + 1, :],
-        lax.broadcasted_iota(I32, (cap, samples), 0))
+    words_copy.wait()
     for s in crosses:
         s.step(0)
     small_come(sm_args, s_core, sm1)
@@ -467,8 +489,11 @@
     def grad_copy(p, slot):
         return remote(slot_grads.at[p], back.at[slot], g_send.at[p], g_recv.at[slot], {"shard": p})
 
+    def plane_to(j):
+        return ((z + far_step(j, nz)) % nz) * ny
+
     def slot_plane(j):
-        first = ((z + plane_step(j, nz)) % nz) * ny
+        first = plane_to(j)
         total = jnp.zeros((ny * cap, 2 * emb), F32)
         for f in range(feats):
             word = words[first // 8, f]
@@ -478,49 +503,21 @@
             part = total[i * cap:(i + 1) * cap]
             slot_grads[first + i] = (part[:, :emb] + part[:, emb:]) * nibble_scale(first + i)
 
+    def send_plane(j):
         @pl.loop(0, ny)
         def _(i):
-            p = first + (yy + i + 1) % ny
+            p = plane_to(j) + (yy + i + 1) % ny
 
             @pl.when(p != me)
             def _():
                 grad_copy(p, me).start()
 
-    @pl.loop(0, nz // 2)
-    def _(j):
-        slot_plane(j)
-
-    for s in tops:
-        s.step(1)
-
-    @pl.loop(nz // 2, nz)
-    def _(j):
-        slot_plane(j)
-
-    back[me] = slot_grads[me]
-
-    for s in crosses:
-        s.step(1)
-    small_come(sm_args, s_x, sm2)
-    sm_args = small_go(2, gy, sm2, s_y)
-    for s in tops:
-        s.step(2)
-    for s in crosses:
-        s.step(2)
-    small_come(sm_args, s_y, sm3)
-    sm_args = small_go(3, gz, sm3, s_z)
-    for s in tops:
-        s.step(3)
-    for s in crosses:
-        s.step(3)
-    for s in tops:
-        s.step(4)
-    for s in crosses:
-        s.step(4)
-    small_come(sm_args, s_z, small_out)
+        @pl.when(j == nz - 1)
+        def _():
+            back[me] = slot_grads[me]
 
     def owner_plane(j):
-        first = plane_from(j, z, nz) * ny
+        first = plane_from(far_step(j, nz), z, nz) * ny
 
         @pl.loop(0, ny)
         def _(i):
@@ -544,18 +541,51 @@
             w = pl.ds(pl.multiple_of(at, mstep), mstep)
             tsum[w] = jnp.where(j == 0, part, tsum[w] + part)
 
-    @pl.loop(0, nz // 2)
-    def _(j):
-        owner_plane(j)
-
-    for s in tops:
-        s.step(5)
-    for s in crosses:
-        s.step(5)
-
-    @pl.loop(nz // 2, nz)
-    def _(j):
-        owner_plane(j)
+    def slot_planes(lo, hi, send):
+        @pl.loop(lo, min(hi, nz))
+        def _(j):
+            slot_plane(j)
+            if send:
+                send_plane(j)
+
+    def send_planes(lo, hi):
+        @pl.loop(lo, min(hi, nz))
+        def _(j):
+            send_plane(j)
+
+    def owner_planes(lo, hi):
+        @pl.loop(lo, min(hi, nz))
+        def _(j):
+            owner_plane(j)
+
+    def steps(which, k):
+        for s in which:
+            s.step(k)
+
+    early = min(3, nz)
+    slot_planes(0, early, True)
+    steps(tops, 1)
+    slot_planes(early, 6, False)
+    steps(tops, 2)
+    slot_planes(min(6, nz), nz, False)
+    steps(crosses, 1)
+    small_come(sm_args, s_x, sm2)
+    sm_args = small_go(2, gy, sm2, s_y)
+    steps(crosses, 2)
+    small_come(sm_args, s_y, sm3)
+    sm_args = small_go(3, gz, sm3, s_z)
+    steps(tops, 3)
+    steps(crosses, 3)
+    send_planes(early, nz)
+    owner_planes(0, early)
+    steps(tops, 4)
+    steps(crosses, 4)
+    steps(tops, 5)
+    steps(crosses, 5)
+    small_come(sm_args, s_z, small_out)
+    owner_planes(early, 5)
+    steps(tops, 6)
+    owner_planes(min(5, nz), nz)
 
     thalf = rows // 2
     tq = thalf // nx
@@ -565,8 +595,6 @@
     sem = lambda k: (t_send.at[k], t_recv.at[k])
     tc = (gc, lambda j: tside(tsum, j), lambda i: rt1, *sem(0))
     pending += spread(*tc)
-    for s in tops:
-        s.step(6)
     arrived(*tc)
     rt1[...] = rt1[...] + tside(tsum, core)[...]
     tx = (gx, lambda j: tpart(rt1, j), lambda i: rt2.at[i], *sem(1))
@@ -597,14 +625,13 @@
         grad_copy(peer_of(k, me, ny, nz), me).wait_send()
 
 
-def dense_and_reduce(x0, slots, lengths, cot, cw, cb, tw, tb, ow, served, nx, ny, rows):
+def dense_and_reduce(x0, words, cot, cw, cb, tw, tb, ow, served, nx, ny, rows):
     samples, width = x0.shape
     top = tw.shape[1]
-    feats, bag, _ = slots.shape
+    feats = words.shape[1]
     n, _, cap = served.shape
     emb = width // feats
     nz = n // ny
-    keys = feats * bag
     vm = pl.BlockSpec(memory_space=pltpu.VMEM)
     v = pltpu.VMEM
     dma = lambda *s: pltpu.SemaphoreType.DMA(s)
@@ -616,25 +643,25 @@
 
     bufs = []
     for r in (r_top, r_cross):
-        for a, b in ((nx, ny), (ny, nx)):
-            q = r // 4
+        for (a, b), q in zip(((nx, ny), (ny, nx)), shares(r, nx, ny)):
             p = q // a
             u = p // b
             bufs += [v(tiles(q, nz), F32), v(tiles(a, p, nz), F32), v(tiles(p, nz), F32),
                      v(tiles(b, u, nz), F32), v(tiles(u, nz), F32), v(tiles(nz, u), F32)]
     sm_bufs = [v((k, *sm), F32) for k in (2, nx, ny, nz)] + [v(sm, F32)] * 3
-    sems = [dma(n), dma(n), dma(4, most), dma(4, most), dma(4, most), dma(4, most), dma(4, 8, most), dma(4, 8, most)]
+    sems = [dma(n), dma(n), dma(4, most), dma(4, most), dma(4, most), dma(4, most), dma(4, 8, most), dma(4, 8, most),
+            pltpu.SemaphoreType.DMA]
     own = [
         v(tiles(r_cross, nz), F32), v(tiles(r_top, nz), F32), v(sm, F32),
         v((n, cap, emb), F32), v((n, cap, emb), F32), v((rows, emb), F32),
         v((rows // 2, emb), F32), v((nx, rows // 2 // nx, emb), F32),
-        v((pl.cdiv(n, 8), feats, cap, samples), I32), v((keys, samples), I32), v((keys, samples), I32),
+        v(words.shape, I32),
         v((samples, width), F32), v((samples, width), BF16), v((samples, top), BF16), v((samples, width), BF16),
         v((samples, width), F32), v((feats, samples, 2 * emb), BF16),
     ]
 
     def body(*refs):
-        head, rest = refs[:15 + len(own)], refs[15 + len(own):]
+        head, rest = refs[:14 + len(own)], refs[14 + len(own):]
         dense_kernel(nx, ny, nz, *head, rest[:24], rest[24:31], rest[31:])
 
     return pl.pallas_call(
@@ -646,13 +673,55 @@
             jax.ShapeDtypeStruct(tiles(r_top, nz), F32),
             jax.ShapeDtypeStruct(sm, F32),
         ],
-        in_specs=[vm] * 10,
+        in_specs=[vm, pl.BlockSpec(memory_space=pl.ANY)] + [vm] * 7,
         out_specs=[vm] * 5,
         scratch_shapes=own + bufs + sm_bufs + sems,
         compiler_params=pltpu.CompilerParams(
             collective_id=1, has_side_effects=True, vmem_limit_bytes=VMEM_LIMIT),
         name="dense_reduce",
-    )(x0, slots, lengths, cot, cw, cb, tw, tb, ow, served)
+    )(x0, words, cot, cw, cb, tw, tb, ow, served)
+
+
+def publish_kernel(pieces, cross, tops, table, small, logits, cross_out, top_out, table_out,
+                   cb_out, tb_out, ow_out, logits_out, cross_buf, top_buf, table_buf, sems):
+    logits_out[...] = logits[...]
+    reads, writes = [], []
+    for src, buf, dst in ((cross, cross_buf, cross_out), (tops, top_buf, top_out), (table, table_buf, table_out)):
+        size = src.shape[0] // pieces
+        for i in range(pieces):
+            w = pl.ds(i * size, size)
+            k = len(reads)
+            reads.append(pltpu.make_async_copy(src.at[w], buf.at[w], sems.at[0, k]))
+            writes.append(pltpu.make_async_copy(buf.at[w], dst.at[w], sems.at[1, k]))
+    for read in reads:
+        read.start()
+    for read, write in zip(reads, writes):
+        read.wait()
+        write.start()
+    at = 0
+    for out in (cb_out, tb_out, ow_out):
+        out[...] = small[pl.ds(at, out.shape[0]), :]
+        at += out.shape[0]
+    for write in writes:
+        write.wait()
+
+
+def publish(cross, tops, table, small, logits, width, top):
+    hbm = pl.BlockSpec(memory_space=pl.ANY)
+    vm = pl.BlockSpec(memory_space=pltpu.VMEM)
+    pieces = 4
+    return pl.pallas_call(
+        functools.partial(publish_kernel, pieces),
+        out_shape=[jax.ShapeDtypeStruct(a.shape, F32) for a in (cross, tops, table)]
+        + [jax.ShapeDtypeStruct((k // 128, 128), F32) for k in (width, top, top)]
+        + [jax.ShapeDtypeStruct(logits.shape, F32)],
+        in_specs=[hbm, hbm, hbm, vm, vm],
+        out_specs=[hbm, hbm, hbm, vm, vm, vm, vm],
+        scratch_shapes=[pltpu.VMEM(a.shape, F32) for a in (cross, tops, table)]
+        + [pltpu.SemaphoreType.DMA((2, 3 * pieces))],
+        compiler_params=pltpu.CompilerParams(vmem_limit_bytes=VMEM_LIMIT),
+        name="publish",
+    )(cross, tops, table, small, logits)
 
 
 def from_tiles(tiles, rows, columns):
@@ -663,13 +732,14 @@
               nx=NX, ny=NY):
     width, top = top_weight.shape
     keys, live = jnp.transpose(slots, (1, 2, 0)), lengths.T
-    x0, served = fetch(wanted[0], table, keys, live, ny)
+    x0, served, words = fetch(wanted[0], table, keys, live, ny)
     logits, table_grad, cross, tops, vecs = dense_and_reduce(
-        x0, keys, live, logit_grad[None], cross_weight, cross_bias[None], top_weight, top_bias[None], out_weight[None],
+        x0, words, logit_grad[None], cross_weight, cross_bias[None], top_weight, top_bias[None], out_weight[None],
         served, nx, ny, table.shape[0])
-    vec = vecs.reshape(-1)
+    cross, tops, table_grad, g_cb, g_tb, g_ow, logits = publish(
+        cross, tops, table_grad, vecs, logits, width, top)
     return (logits[0], from_tiles(cross, width, width), from_tiles(tops, width, top),
-            vec[:width], vec[width:width + top], vec[width + top:], table_grad)
+            g_cb.reshape(-1), g_tb.reshape(-1), g_ow.reshape(-1), table_grad)
 
 
 def solution(mesh):

time: 222 us -> 205 us (0.923)
  local copies, waits for them, and re-layouts: 11.7 us -> 0 us
  Pallas kernels: 209 us -> 204 us
    unnamed x8 -> x0, local copies, waits for them, and re-layouts: 9.12 us -> none
    pallas_call x0 -> x1, Pallas kernels: none -> 7.31 us  [publish(): pl.pallas_call(functools.partial(publish_kernel, pieces), out_shape=[jax....]
    pallas_call x1, Pallas kernels: 76.7 us -> 69.6 us  [fetch(): pl.pallas_call(functools.partial(fetch_kernel, n, ny), out_shape=[jax.Sha...]
    pallas_call x1, Pallas kernels: 133 us -> 127 us  [dense_and_reduce(): pl.pallas_call(body, out_shape=[jax.ShapeDtypeStruct((1, samples), F32),...]
    slice x2 -> x0, local copies, waits for them, and re-layouts: 2.61 us -> none  [the longest x1 1.33 us: on_device(): vec[width + top:]]
where the time goes in v4:
time: 205 us
  Pallas kernels  204 us (100%)
    pallas_call x1, Pallas kernels, dense_and_reduce(): pl.pallas_call(body, out_shape=[jax.ShapeDtypeStruct((1, samples), F32),...  127 us
    pallas_call x1, Pallas kernels, fetch(): pl.pallas_call(functools.partial(fetch_kernel, n, ny), out_shape=[jax.Sha...  69.6 us
    pallas_call x1, Pallas kernels, publish(): pl.pallas_call(functools.partial(publish_kernel, pieces), out_shape=[jax....  7.31 us

profile of v4, /device:TPU:1, one launch (start us, length us, event | category | flops | bytes accessed | tf_op | source)
XLA Modules:
  0.0 204.9 jit_solution(15784213617811182257)
XLA Ops:
  0.6 69.6 %fetch_pool.1 = (bf16[512,1024]{1,0:T(8,128)(2,1)}, s32[32,1,128]{2,1,0:T(1,128)}, s32[4,8,128,512]{3,2,1,0:T(8,128)}) custom-call(s32[32,1,128]{2,1,0:T(1,128)} %bitcast.20, f32[2048,128]{1,0:T(8,128)} %table.1, s32[8,4,512]{2,1,0:T(4,128)} %bitcast.19, s32[8,512]{1,0:T(8,128)} %bitcast.21), custom_call_target="tpu_custom_call" | custom-call | tf_op jit(solution)/shard_map/fetch_pool/pallas_call | solution.py:222
  70.3 127.1 %dense_reduce.1 = (f32[1,512]{1,0:T(1,128)}, f32[2048,128]{1,0:T(8,128)}, f32[128,8,8,128]{3,2,1,0:T(8,128)}, f32[64,8,8,128]{3,2,1,0:T(8,128)}, f32[16,128]{1,0:T(8,128)}) custom-call(bf16[512,1024]{1,0:T(8,128)(2,1)} %get-tuple-element.22.refs_0_, s32[4,8,128,512]{3,2,1,0:T(8,128)} %get-tuple-element.23.refs_1_, f32[1,512]{1,0:T(1,128)} %bitcast.23, ...), custom_call_target="tpu_custom_call" | custom-call | tf_op jit(solution)/shard_map/dense_reduce/pallas_call | solution.py:667
  197.4 7.3 %publish.1 = (f32[128,8,8,128]{3,2,1,0:T(8,128)}, f32[64,8,8,128]{3,2,1,0:T(8,128)}, f32[2048,128]{1,0:T(8,128)}, f32[8,128]{1,0:T(8,128)}, f32[4,128]{1,0:T(4,1...) custom-call(f32[128,8,8,128]{3,2,1,0:T(8,128)} %get-tuple-element.25.cross, f32[64,8,8,128]{3,2,1,0:T(8,128)} %get-tuple-element.26.tops, ...), custom_call_target="tpu_custom_call" | custom-call | tf_op jit(solution)/shard_map/publish/pallas_call | solution.py:713

commit v5 on v4

--- a/solution.py
+++ b/solution.py
@@ -78,6 +78,9 @@
 
 
 def far_step(j, nz):
+    if nz == 8:
+        q = (j + 1) // 2
+        return (4 + (q * q * q + 3 * q * q + 3 * q) % 5 * (1 - 2 * (j % 2))) % 8
     return nz // 2 + (j // 2 + j % 2) * (1 - 2 * (j % 2))
 
 
@@ -263,7 +266,7 @@
 def shares(r, nx, ny):
     per = r // 2
     unit = nx * ny
-    second = max(unit, per // 4 // unit * unit)
+    second = max(unit, per // 2 // unit * unit)
     return per - second, second
 
 
@@ -344,7 +347,8 @@
 
 
 def dense_kernel(nx, ny, nz, x0, words_in, cot, cw, cb, tw, tb, ow, served,
-                 logits, table_out, cross_out, top_out, small_out,
+                 logits, table_out, cross_hbm, top_hbm, small_out,
+                 cross_out, top_out,
                  g_cross, g_top, small, slot_grads, back, tsum, rt1, rt2,
                  words, y, h, dzb, dyb, dh, dxhl, bufs, sm_bufs, sems):
     n = ny * nz
@@ -358,7 +362,7 @@
     gy = Group(ny, yy, lambda j: {"shard": z * ny + j})
     gz = Group(nz, z, lambda j: {"shard": j * ny + yy})
     gc = Group(2, core, lambda j: {"dp": x * 2 + j})
-    g_send, g_recv, t_send, t_recv, sm_send, sm_recv, d_send, d_recv, words_sem = sems
+    g_send, g_recv, t_send, t_recv, sm_send, sm_recv, d_send, d_recv, words_sem, out_sems = sems
     words_copy = pltpu.make_async_copy(words_in, words, words_sem)
     words_copy.start()
 
@@ -565,21 +569,22 @@
     early = min(3, nz)
     slot_planes(0, early, True)
     steps(tops, 1)
-    slot_planes(early, 6, False)
-    steps(tops, 2)
-    slot_planes(min(6, nz), nz, False)
+    slot_planes(early, 5, False)
     steps(crosses, 1)
     small_come(sm_args, s_x, sm2)
     sm_args = small_go(2, gy, sm2, s_y)
+    steps(tops, 2)
+    slot_planes(min(5, nz), 7, False)
     steps(crosses, 2)
     small_come(sm_args, s_y, sm3)
     sm_args = small_go(3, gz, sm3, s_z)
+    slot_planes(min(7, nz), nz, False)
     steps(tops, 3)
     steps(crosses, 3)
     send_planes(early, nz)
-    owner_planes(0, early)
     steps(tops, 4)
     steps(crosses, 4)
+    owner_planes(0, early)
     steps(tops, 5)
     steps(crosses, 5)
     small_come(sm_args, s_z, small_out)
@@ -610,12 +615,17 @@
     there = lambda i: rows_at(table_out, core * thalf + i * tq, tq)
     tb_ = (gx, lambda j: there(x), there, *sem(2))
     pending += spread(*tb_)
+    flushes = []
+    for i, (which, src, dst) in enumerate(((tops, top_out, top_hbm), (crosses, cross_out, cross_hbm))):
+        steps(which, 7)
+        flushes.append(pltpu.make_async_copy(src, dst, out_sems.at[i]))
+        flushes[-1].start()
     arrived(*tb_)
     tcb = (gc, lambda j: tside(table_out, core), lambda i: tside(table_out, i), *sem(3))
     pending += spread(*tcb)
-    for s in streams:
-        s.step(7)
     arrived(*tcb)
+    for cp in flushes:
+        cp.wait()
 
     for cp in pending + [cp for s in streams for cp in s.pending]:
         cp.wait_send()
@@ -650,8 +660,9 @@
                      v(tiles(b, u, nz), F32), v(tiles(u, nz), F32), v(tiles(nz, u), F32)]
     sm_bufs = [v((k, *sm), F32) for k in (2, nx, ny, nz)] + [v(sm, F32)] * 3
     sems = [dma(n), dma(n), dma(4, most), dma(4, most), dma(4, most), dma(4, most), dma(4, 8, most), dma(4, 8, most),
-            pltpu.SemaphoreType.DMA]
+            pltpu.SemaphoreType.DMA, dma(2)]
     own = [
+        v(tiles(r_cross, nz), F32), v(tiles(r_top, nz), F32),
         v(tiles(r_cross, nz), F32), v(tiles(r_top, nz), F32), v(sm, F32),
         v((n, cap, emb), F32), v((n, cap, emb), F32), v((rows, emb), F32),
         v((rows // 2, emb), F32), v((nx, rows // 2 // nx, emb), F32),
@@ -674,7 +685,7 @@
             jax.ShapeDtypeStruct(sm, F32),
         ],
         in_specs=[vm, pl.BlockSpec(memory_space=pl.ANY)] + [vm] * 7,
-        out_specs=[vm] * 5,
+        out_specs=[vm, vm, pl.BlockSpec(memory_space=pl.ANY), pl.BlockSpec(memory_space=pl.ANY), vm],
         scratch_shapes=own + bufs + sm_bufs + sems,
         compiler_params=pltpu.CompilerParams(
             collective_id=1, has_side_effects=True, vmem_limit_bytes=VMEM_LIMIT),

time: 205 us -> 195 us (0.951)
  Pallas kernels: 204 us -> 192 us
    pallas_call x1, Pallas kernels: 127 us -> 115 us  [dense_and_reduce(): pl.pallas_call(body, out_shape=[jax.ShapeDtypeStruct((1, samples), F32),...]
where the time goes in v5:
time: 195 us; the launch traced here: 193 us
  Pallas kernels  192 us (98%)
    pallas_call x1, Pallas kernels, dense_and_reduce(): pl.pallas_call(body, out_shape=[jax.ShapeDtypeStruct((1, samples), F32),...  115 us
    pallas_call x1, Pallas kernels, fetch(): pl.pallas_call(functools.partial(fetch_kernel, n, ny), out_shape=[jax.Sha...  69.6 us
    pallas_call x1, Pallas kernels, publish(): pl.pallas_call(functools.partial(publish_kernel, pieces), out_shape=[jax....  7.31 us

profile of v5, /device:TPU:1, one launch (start us, length us, event | category | flops | bytes accessed | tf_op | source)
XLA Modules:
  0.0 193.0 jit_solution(12066828917959997082)
XLA Ops:
  0.6 69.6 %fetch_pool.1 = (bf16[512,1024]{1,0:T(8,128)(2,1)}, s32[32,1,128]{2,1,0:T(1,128)}, s32[4,8,128,512]{3,2,1,0:T(8,128)}) custom-call(s32[32,1,128]{2,1,0:T(1,128)} %bitcast.20, f32[2048,128]{1,0:T(8,128)} %table.1, s32[8,4,512]{2,1,0:T(4,128)} %bitcast.19, s32[8,512]{1,0:T(8,128)} %bitcast.21), custom_call_target="tpu_custom_call" | custom-call | tf_op jit(solution)/shard_map/fetch_pool/pallas_call | solution.py:225
  70.3 115.2 %dense_reduce.1 = (f32[1,512]{1,0:T(1,128)}, f32[2048,128]{1,0:T(8,128)}, f32[128,8,8,128]{3,2,1,0:T(8,128)}, f32[64,8,8,128]{3,2,1,0:T(8,128)}, f32[16,128]{1,0:T(8,128)}) custom-call(bf16[512,1024]{1,0:T(8,128)(2,1)} %get-tuple-element.22.refs_0_, s32[4,8,128,512]{3,2,1,0:T(8,128)} %get-tuple-element.23.refs_1_, f32[1,512]{1,0:T(1,128)} %bitcast.23, ...), custom_call_target="tpu_custom_call" | custom-call | tf_op jit(solution)/shard_map/dense_reduce/pallas_call | solution.py:678
  185.5 7.3 %publish.1 = (f32[128,8,8,128]{3,2,1,0:T(8,128)}, f32[64,8,8,128]{3,2,1,0:T(8,128)}, f32[2048,128]{1,0:T(8,128)}, f32[8,128]{1,0:T(8,128)}, f32[4,128]{1,0:T(4,1...) custom-call(f32[128,8,8,128]{3,2,1,0:T(8,128)} %get-tuple-element.25.cross, f32[64,8,8,128]{3,2,1,0:T(8,128)} %get-tuple-element.26.tops, ...), custom_call_target="tpu_custom_call" | custom-call | tf_op jit(solution)/shard_map/publish/pallas_call | solution.py:724

commit v6 on v5

--- a/solution.py
+++ b/solution.py
@@ -569,16 +569,16 @@
     early = min(3, nz)
     slot_planes(0, early, True)
     steps(tops, 1)
-    slot_planes(early, 5, False)
+    slot_planes(early, 4, False)
     steps(crosses, 1)
     small_come(sm_args, s_x, sm2)
     sm_args = small_go(2, gy, sm2, s_y)
     steps(tops, 2)
-    slot_planes(min(5, nz), 7, False)
+    slot_planes(min(4, nz), 6, False)
     steps(crosses, 2)
     small_come(sm_args, s_y, sm3)
     sm_args = small_go(3, gz, sm3, s_z)
-    slot_planes(min(7, nz), nz, False)
+    slot_planes(min(6, nz), nz, False)
     steps(tops, 3)
     steps(crosses, 3)
     send_planes(early, nz)

time: 195 us -> 196 us (level)
  no operation moved by 1% of the time
where the time goes in v6:
time: 196 us; the launch traced here: 194 us
  Pallas kernels  193 us (98%)
    pallas_call x1, Pallas kernels, dense_and_reduce(): pl.pallas_call(body, out_shape=[jax.ShapeDtypeStruct((1, samples), F32),...  116 us
    pallas_call x1, Pallas kernels, fetch(): pl.pallas_call(functools.partial(fetch_kernel, n, ny), out_shape=[jax.Sha...  69.6 us
    pallas_call x1, Pallas kernels, publish(): pl.pallas_call(functools.partial(publish_kernel, pieces), out_shape=[jax....  7.31 us

profile of v6, /device:TPU:1, one launch (start us, length us, event | category | flops | bytes accessed | tf_op | source)
XLA Modules:
  0.0 194.0 jit_solution(15317155803837687879)
XLA Ops:
  0.6 69.6 %fetch_pool.1 = (bf16[512,1024]{1,0:T(8,128)(2,1)}, s32[32,1,128]{2,1,0:T(1,128)}, s32[4,8,128,512]{3,2,1,0:T(8,128)}) custom-call(s32[32,1,128]{2,1,0:T(1,128)} %bitcast.20, f32[2048,128]{1,0:T(8,128)} %table.1, s32[8,4,512]{2,1,0:T(4,128)} %bitcast.19, s32[8,512]{1,0:T(8,128)} %bitcast.21), custom_call_target="tpu_custom_call" | custom-call | tf_op jit(solution)/shard_map/fetch_pool/pallas_call | solution.py:225
  70.3 116.2 %dense_reduce.1 = (f32[1,512]{1,0:T(1,128)}, f32[2048,128]{1,0:T(8,128)}, f32[128,8,8,128]{3,2,1,0:T(8,128)}, f32[64,8,8,128]{3,2,1,0:T(8,128)}, f32[16,128]{1,0:T(8,128)}) custom-call(bf16[512,1024]{1,0:T(8,128)(2,1)} %get-tuple-element.22.refs_0_, s32[4,8,128,512]{3,2,1,0:T(8,128)} %get-tuple-element.23.refs_1_, f32[1,512]{1,0:T(1,128)} %bitcast.23, ...), custom_call_target="tpu_custom_call" | custom-call | tf_op jit(solution)/shard_map/dense_reduce/pallas_call | solution.py:678
  186.5 7.3 %publish.1 = (f32[128,8,8,128]{3,2,1,0:T(8,128)}, f32[64,8,8,128]{3,2,1,0:T(8,128)}, f32[2048,128]{1,0:T(8,128)}, f32[8,128]{1,0:T(8,128)}, f32[4,128]{1,0:T(4,1...) custom-call(f32[128,8,8,128]{3,2,1,0:T(8,128)} %get-tuple-element.25.cross, f32[64,8,8,128]{3,2,1,0:T(8,128)} %get-tuple-element.26.tops, ...), custom_call_target="tpu_custom_call" | custom-call | tf_op jit(solution)/shard_map/publish/pallas_call | solution.py:724
